TPU v7x, 256 devices: a whole 4x4x8 slice. The times are simulated.
256 devices in a mesh: group: 8 (over y, core), dom: 32 (over z, x).
Axes of the slice: x: 4, y: 4, z: 8, core: 2. Of those that a mesh axis runs over, the one named last changes fastest.
Arguments:
- node_feats: bfloat16 [524288, 512], P(('group', 'dom')), may hold values from -36 to 36
- send_rows: int32 [256, 32, 32], P(('group', 'dom')), may hold values from 0 to 2047
- hub_rows: int32 [256, 8], P(('group', 'dom')), may hold values from 0 to 2047
- neighbours: int32 [524288, 16], P(('group', 'dom')), may hold values from 0 to 5119, as said below
- w_self: bfloat16 [512, 512], replicated, may hold values from -0.25 to 0.25
- w_neigh: bfloat16 [512, 512], replicated, may hold values from -0.25 to 0.25
- w_head: bfloat16 [512, 128], replicated, may hold values from -1.5 to 1.5
- s_first: bfloat16 [512, 512], replicated, may hold values from -0.25 to 0.25
- s_second: bfloat16 [512, 128], replicated, may hold values from -1.5 to 1.5
Outputs:
- teacher_hidden: bfloat16 [524288, 512], P(('group', 'dom'))
- grad_first: float32 [512, 512], replicated
- grad_second: float32 [512, 128], replicated
Inputs may be any that keep to these rules, and one draw needn't show every extreme that they name: `neighbours`: entries below 2048 are local rows; entries from 2048 to 3071 name halo rows, and from a given peer only its first rows, up to 32; the rest name hubs.
All inputs are finite; a program needn't handle non-finite values.
Results may differ from a plain program's by a relative error of at most 0.0025.
Values may be sent and summed in bfloat16 or wider, within the bound.
No kernel may reach another device: no remote copies, remote signals or barrier semaphores. Data moves between devices by JAX's collectives and lax.ppermute only.
A program may use at most 128 MiB of HBM per device.

v0:
```python
import functools

import jax
import jax.numpy as jnp
from jax import lax
from jax.experimental import pallas as pl
from jax.experimental.pallas import tpu as pltpu
from jax.sharding import Mesh
from jax.sharding import PartitionSpec as P

DEG = 16
TEMPER = 2.0
NY, NC, NZ, NX = 4, 2, 8, 4
ALL = ("y", "core", "z", "x")
DOM = ("z", "x")
PLANE = ("y", "x")
BF = jnp.bfloat16
F32 = jnp.float32
LAST = jnp.float32
NT = (((1,), (1,)), ((), ()))
TN = (((0,), (0,)), ((), ()))

ROWS = 2048
WIDTH = 512
PEERS = 32
CAP = 32
HUBD = 8
SLOT = CAP + HUBD
LO = 256
LOCAL_HI = ROWS // LO
REM_HI = 12
GROUP = 16
TILE = 512
VMEM = 60 << 20
UNROLL = 2


def onehot(cond):
    return jnp.where(cond, 1.0, 0.0).astype(BF)


def params():
    return pltpu.CompilerParams(dimension_semantics=("arbitrary",), vmem_limit_bytes=VMEM)


def plain():
    return pltpu.CompilerParams(vmem_limit_bytes=VMEM)


def pick_kernel(rows_ref, hub_ref, x_ref, out_ref):
    x = x_ref[...]
    rows_t = rows_ref[...].T
    lane = lax.broadcasted_iota(jnp.int32, (CAP, ROWS), 1)
    per = 8
    hub_t = hub_ref[...].T
    hub_lane = lax.broadcasted_iota(jnp.int32, (HUBD, ROWS), 1)
    hubs = jnp.dot(onehot(hub_t[:, 0:1] == hub_lane), x, preferred_element_type=F32).astype(BF)
    for block in range(PEERS // per):
        picks = jnp.concatenate(
            [onehot(rows_t[:, s : s + 1] == lane) for s in range(block * per, (block + 1) * per)], axis=0
        )
        got = jnp.dot(picks, x, preferred_element_type=F32).astype(BF)
        for n in range(per):
            out_ref[block * per + n, 0:CAP, :] = got[n * CAP : (n + 1) * CAP, :]
            out_ref[block * per + n, CAP:SLOT, :] = hubs


def pick_rows(feats, send_rows, hub_rows):
    return pl.pallas_call(
        pick_kernel,
        out_shape=jax.ShapeDtypeStruct((PEERS, SLOT, WIDTH), BF),
        compiler_params=plain(),
        cost_estimate=pl.CostEstimate(flops=3_000_000_000, bytes_accessed=3_000_000, transcendentals=0),
        name="pick_rows",
    )(send_rows, hub_rows, feats)


def count_kernel(idx_ref, xall_ref, agg_ref, rem_ref, loc_ref):
    high = (LOCAL_HI + REM_HI) * GROUP
    left_row = lax.broadcasted_iota(jnp.int32, (high, LO), 0)
    low_row = lax.broadcasted_iota(jnp.int32, (LO, LO), 0)
    node = lax.broadcasted_iota(jnp.int32, (1, LO), 1) // DEG

    def build(g, carry):
        idx = idx_ref[pl.ds(g, 1), :]
        where_hi = (idx // LO) * GROUP + node
        where_lo = idx % LO
        left = onehot(jnp.broadcast_to(where_hi, (high, LO)) == left_row)
        low = onehot(jnp.broadcast_to(where_lo, (LO, LO)) == low_row)
        counts = lax.dot_general(left, low, NT, preferred_element_type=F32).astype(BF)
        at = pl.ds(pl.multiple_of(g * GROUP, GROUP), GROUP)
        for h in range(LOCAL_HI):
            loc_ref[at, h * LO : (h + 1) * LO] = counts[h * GROUP : (h + 1) * GROUP, :]
        for h in range(REM_HI):
            r = (LOCAL_HI + h) * GROUP
            rem_ref[at, h * LO : (h + 1) * LO] = counts[r : r + GROUP, :]
        return carry

    lax.fori_loop(0, TILE // GROUP, build, 0, unroll=UNROLL)
    agg_ref[...] = jnp.dot(loc_ref[...], xall_ref[...], preferred_element_type=F32)


def count_part(idx, feats):
    rem = REM_HI * LO
    return pl.pallas_call(
        count_kernel,
        grid=(ROWS // TILE,),
        in_specs=[pl.BlockSpec((TILE // GROUP, LO), lambda i: (i, 0)), whole((ROWS, WIDTH))],
        out_specs=[tile(WIDTH), tile(rem)],
        out_shape=[jax.ShapeDtypeStruct((ROWS, WIDTH), F32), jax.ShapeDtypeStruct((ROWS, rem), BF)],
        scratch_shapes=[pltpu.VMEM((TILE, ROWS), BF)],
        compiler_params=params(),
        cost_estimate=pl.CostEstimate(flops=25_000_000_000, bytes_accessed=20_000_000, transcendentals=0),
        name="count_part",
    )(idx, feats)


def soft(logits):
    scaled = logits / TEMPER
    e = jnp.exp(scaled - jnp.max(scaled, axis=-1, keepdims=True))
    return e / jnp.sum(e, axis=-1, keepdims=True)


def dense_kernel(x_ref, wself_ref, sfirst_ref, ssecond_ref, base_ref, sh_ref, ps_ref):
    x = x_ref[...]
    base_ref[...] = jnp.dot(x, wself_ref[...], preferred_element_type=F32)
    hidden = jnp.maximum(jnp.dot(x, sfirst_ref[...], preferred_element_type=F32), 0.0).astype(BF)
    sh_ref[...] = hidden
    ps_ref[...] = soft(jnp.dot(hidden, ssecond_ref[...], preferred_element_type=F32))


def whole(shape):
    return pl.BlockSpec(shape, lambda i: (0,) * len(shape), pipeline_mode=pl.Buffered(1))


def tile(n):
    return pl.BlockSpec((TILE, n), lambda i: (i, 0))


def dense_part(feats, w_self, s_first, s_second):
    return pl.pallas_call(
        dense_kernel,
        grid=(ROWS // TILE,),
        in_specs=[tile(WIDTH), whole((WIDTH, WIDTH)), whole((WIDTH, WIDTH)), whole((WIDTH, 128))],
        out_specs=[tile(WIDTH), tile(WIDTH), tile(128)],
        out_shape=[
            jax.ShapeDtypeStruct((ROWS, WIDTH), F32),
            jax.ShapeDtypeStruct((ROWS, WIDTH), BF),
            jax.ShapeDtypeStruct((ROWS, 128), F32),
        ],
        compiler_params=params(),
        cost_estimate=pl.CostEstimate(flops=3_000_000_000, bytes_accessed=10_000_000, transcendentals=0),
        name="dense_part",
    )(feats, w_self, s_first, s_second)


def tail_kernel(
    scale, pos_ref, agg_ref, rem_ref, base_ref, sh_ref, ps_ref, x_ref, r_ref, p1, p2, p3, p4, p5, p6, p7,
    wneigh_ref, whead_ref, ssecond_ref, hid_ref, keep_ref, send_ref, g_ref,
):
    step = pl.program_id(0)

    @pl.when(step == 0)
    def _():
        g_ref[...] = jnp.zeros_like(g_ref)

    first = PEERS * SLOT
    acc = agg_ref[...] + jnp.dot(rem_ref[:, 0:first], r_ref[...], preferred_element_type=F32)
    for n, part in enumerate((p1, p2, p3, p4, p5, p6, p7)):
        at = first + n * LO
        acc = acc + jnp.dot(rem_ref[:, at : at + LO], part[...], preferred_element_type=F32)
    agg = (acc / DEG).astype(BF)
    pre = base_ref[...] + jnp.dot(agg, wneigh_ref[...], preferred_element_type=F32)
    hidden = jnp.maximum(pre, 0.0).astype(BF)
    hid_ref[...] = hidden
    teach = soft(jnp.dot(hidden, whead_ref[...], preferred_element_type=F32))
    delta = (TEMPER * (ps_ref[...] - teach) * scale).astype(BF)
    sh = sh_ref[...]
    back = lax.dot_general(delta, ssecond_ref[...], NT, preferred_element_type=F32)
    back = jnp.where(sh.astype(F32) > 0.0, back, 0.0).astype(BF)
    first_grad = lax.dot_general(x_ref[...], back, TN, preferred_element_type=F32)
    for c in range(4):
        g_ref[c * WIDTH : (c + 1) * WIDTH, :] += first_grad[:, c * 128 : (c + 1) * 128]
    g_ref[4 * WIDTH : 5 * WIDTH, :] += lax.dot_general(sh, delta, TN, preferred_element_type=F32)

    @pl.when(step == pl.num_programs(0) - 1)
    def _():
        core = pos_ref[1]
        keep_ref[...] = g_ref[pl.ds(pl.multiple_of(core * HALF, 8), HALF), :]
        send_ref[...] = g_ref[pl.ds(pl.multiple_of((1 - core) * HALF, 8), HALF), :]


SMEM_SPEC = pl.BlockSpec(memory_space=pltpu.SMEM)


def tail_part(scale, pos, agg, rem, base, sh, ps, feats, got, parts, w_neigh, w_head, s_second):
    fixed = pl.BlockSpec((HALF, 128), lambda i: (0, 0))
    return pl.pallas_call(
        functools.partial(tail_kernel, scale),
        grid=(ROWS // TILE,),
        in_specs=[
            SMEM_SPEC, tile(WIDTH), tile(REM_HI * LO), tile(WIDTH), tile(WIDTH), tile(128), tile(WIDTH),
            whole((PEERS * SLOT, WIDTH)),
        ]
        + [whole((LO, WIDTH))] * 7
        + [whole((WIDTH, WIDTH)), whole((WIDTH, 128)), whole((WIDTH, 128))],
        out_specs=[tile(WIDTH), fixed, fixed],
        out_shape=[
            jax.ShapeDtypeStruct((ROWS, WIDTH), BF),
            jax.ShapeDtypeStruct((HALF, 128), F32),
            jax.ShapeDtypeStruct((HALF, 128), F32),
        ],
        scratch_shapes=[pltpu.VMEM((2 * HALF, 128), F32)],
        compiler_params=params(),
        cost_estimate=pl.CostEstimate(flops=10_000_000_000, bytes_accessed=30_000_000, transcendentals=0),
        name="tail_part",
    )(pos, agg, rem, base, sh, ps, feats, got, *parts, w_neigh, w_head, s_second)


HALF = 5 * WIDTH // 2


def unpack_kernel(pos_ref, mine_ref, other_ref, first, second, g_ref):
    core = pos_ref[1]
    g_ref[pl.ds(pl.multiple_of(core * HALF, 16), HALF), :] = mine_ref[...].astype(F32)
    g_ref[pl.ds(pl.multiple_of((1 - core) * HALF, 16), HALF), :] = other_ref[...].astype(F32)
    for c in range(4):
        first[:, c * 128 : (c + 1) * 128] = g_ref[c * WIDTH : (c + 1) * WIDTH, :]
    second[...] = g_ref[4 * WIDTH : 5 * WIDTH, :]


def unpack(pos, mine, other):
    vmem = pl.BlockSpec(memory_space=pltpu.VMEM)
    return pl.pallas_call(
        unpack_kernel,
        in_specs=[SMEM_SPEC, vmem, vmem],
        out_specs=[vmem, vmem],
        out_shape=[jax.ShapeDtypeStruct((WIDTH, WIDTH), F32), jax.ShapeDtypeStruct((WIDTH, 128), F32)],
        scratch_shapes=[pltpu.VMEM((2 * HALF, 128), F32)],
        compiler_params=pltpu.CompilerParams(vmem_limit_bytes=16 << 20),
        name="unpack",
    )(pos, mine, other)


def shift(x, axis, n, k):
    return lax.ppermute(x, axis, [(i, (i + k) % n) for i in range(n)])


def swap(x):
    return lax.ppermute(x, "core", [(0, 1), (1, 0)])


def reduce_grads(pos, keep, send):
    total = keep + swap(send)
    plane = NY * NX
    piece = HALF // plane
    part = jnp.sum(a2a(total, PLANE).reshape(plane, piece, 128), axis=0)
    part = jnp.sum(a2a(copies(part, NZ), "z").reshape(NZ, piece, 128), axis=0)
    mine = a2a(copies(part.astype(LAST), plane), PLANE)
    return unpack(pos, mine, swap(mine))


def remap(neighbours, y, c):
    halo = neighbours - ROWS
    halo_at = ROWS + (halo // CAP) * SLOT + halo % CAP
    hub = halo - PEERS * CAP
    inner = hub % LO
    block = hub // LO
    other = ((block % 2) ^ c) * NY + (y - block // 2) % NY
    own_at = ROWS + (inner // HUBD) * SLOT + CAP + inner % HUBD
    far_at = ROWS + PEERS * SLOT + (other - 1) * LO + inner
    hub_at = jnp.where(other == 0, own_at, far_at)
    out = jnp.where(halo < 0, neighbours, jnp.where(hub < 0, halo_at, hub_at))
    return out.reshape(ROWS // GROUP, GROUP * DEG)


def a2a(x, axes):
    return lax.all_to_all(x, axes, split_axis=0, concat_axis=0, tiled=True)


def copies(x, n):
    return jnp.broadcast_to(x[None], (n,) + x.shape).reshape((n * x.shape[0],) + x.shape[1:])


def body(feats, send_rows, hub_rows, neighbours, w_self, w_neigh, w_head, s_first, s_second):
    y = lax.axis_index("y")
    c = lax.axis_index("core")
    pos = jnp.stack([y, c, lax.axis_index("z"), lax.axis_index("x")]).astype(jnp.int32)
    scale = 1.0 / float(ROWS * NY * NC * NZ * NX) ** 0.5

    out = pick_rows(feats, send_rows[0], hub_rows)
    idx = remap(neighbours, y, c)
    got = a2a(out, DOM)
    agg, rem = count_part(idx, feats)
    own = got[:, CAP:SLOT, :].reshape(LO, WIDTH)
    ring = [own] + [shift(own, "y", NY, k) for k in range(1, NY)]
    base, sh, ps = dense_part(feats, w_self, s_first, s_second)
    cross = [swap(r) for r in ring]
    hidden, keep, send = tail_part(
        scale, pos, agg, rem, base, sh, ps, feats, got.reshape(PEERS * SLOT, WIDTH), ring[1:] + cross,
        w_neigh, w_head, s_second,
    )
    grad_first, grad_second = reduce_grads(pos, keep, send)
    return hidden, grad_first, grad_second


def solution(mesh):
    inner = Mesh(mesh.devices.reshape(NY, NC, NZ, NX), ALL)
    return jax.shard_map(
        body,
        mesh=inner,
        in_specs=(P(ALL, None), P(ALL, None, None), P(ALL, None), P(ALL, None), P(), P(), P(), P(), P()),
        out_specs=(P(ALL, None), P(), P()),
        check_vma=False,
    )
```

profile of v0, /device:TPU:2, one launch (start us, length us, event | category | flops | bytes accessed | tf_op | source)
XLA Modules:
  0.0 168.9 jit_solution(8633584626921575158)
XLA Ops:
  0.6 5.4 %pick_rows.1 = bf16[32,40,512]{2,1,0:T(8,128)(2,1)} custom-call(s32[32,32]{1,0:T(8,128)} %bitcast.14, s32[1,8]{1,0:T(1,128)} %hub_ref.1, bf16[2048,512]{1,0:T(8,128)(2,1)} %x_ref.5), custom_call_target="tpu_custom_call" | custom-call | flops 3000000000 | bytes 3000000 | tf_op jit(solution)/shard_map/pick_rows/pallas_call | solution.py:69
  6.0 0.0 copy-start.2
  6.0 11.7 %all-to-all-start = ((bf16[32,40,512]{2,1,0:T(8,128)(2,1)}), bf16[32,40,512]{2,1,0:T(8,128)(2,1)S(1)}, u32[]{:S(2)}, u32[]{:S(2)}) async-start(bf16[32,40,512]{2,1,0:T(8,128)(2,1)} %pick_rows.1), calls=%async_computation | async-start | bytes 2621440 | tf_op jit(solution)/shard_map/all_to_all | solution.py:278
  17.8 0.0 copy-done.2
  17.8 0.6 fusion.4
  18.4 0.3 copy.14
  18.7 1.1 reshape.31.idx_ref
  19.8 30.9 %all-to-all-done = bf16[32,40,512]{2,1,0:T(8,128)(2,1)S(1)} async-done(((bf16[32,40,512]{2,1,0:T(8,128)(2,1)}), bf16[32,40,512]{2,1,0:T(8,128)(2,1)S(1)}, u32[]{:S(2)}, u32[]{:S(2)}) %all-to-all-start) | async-done | bytes 1310752 | tf_op jit(solution)/shard_map/all_to_all | solution.py:278
  50.7 3.1 %collective-permute-start.2 = (bf16[256,512]{1,0:T(8,128)(2,1)S(1)}, bf16[256,512]{1,0:T(8,128)(2,1)S(1)}, u32[]{:S(2)}, u32[]{:S(2)}) collective-permute-start(bf16[256,512]{1,0:T(8,128)(2,1)S(1)} %slice_bitcast_fusion), channel_id=1, source_target_pairs={{0,192},{64,0},{128,64},{192,128},{1,193},{65,1},{129,65},{193,129... | collective-permute-start | bytes 786440 | tf_op jit(solution)/shard_map/ppermute | solution.py:246
  53.8 0.6 collective-permute-start.1
  54.4 1.0 collective-permute-start
  55.4 27.3 %count_part.1 = (f32[2048,512]{1,0:T(8,128)}, bf16[2048,3072]{1,0:T(8,128)(2,1)}) custom-call(s32[128,256]{1,0:T(8,128)} %reshape.31.idx_ref, bf16[2048,512]{1,0:T(8,128)(2,1)} %x_ref.5), custom_call_target="tpu_custom_call" | custom-call | flops 24999999488 | bytes 20000000 | tf_op jit(solution)/shard_map/count_part/pallas_call | solution.py:105
  82.7 0.0 copy-done.1
  82.7 0.6 pad_add_fusion.pos_ref
  83.3 0.0 collective-permute-start.3
  83.3 0.0 collective-permute-done.2.p3
  83.3 0.5 collective-permute-start.6
  83.8 0.0 collective-permute-done.1.p2
  83.8 0.1 collective-permute-start.5
  83.9 0.0 collective-permute-done.p1
  83.9 0.4 collective-permute-start.4
  84.3 7.2 %dense_part.1 = (f32[2048,512]{1,0:T(8,128)}, bf16[2048,512]{1,0:T(8,128)(2,1)}, f32[2048,128]{1,0:T(8,128)}) custom-call(bf16[2048,512]{1,0:T(8,128)(2,1)} %x_ref.5, bf16[512,512]{1,0:T(8,128)(2,1)} %wself_ref.1, bf16[512,512]{1,0:T(8,128)(2,1)} %sfirst_ref.1, bf16[512,128]{1,0:T(8,128)(2,1)} %ssecond_ref.3), custom_call_target="tpu_custom_call" | custom-call | flops 3000000000 | bytes 10000000 | tf_op jit(solution)/shard_map/dense_part/pallas_call | solution.py:141
  91.5 0.0 copy-done.3
  91.5 0.0 copy-done.4
  91.5 0.0 copy-done.5
  91.5 0.0 collective-permute-done.3.p4
  91.6 0.0 copy-start.6
  91.6 0.0 collective-permute-done.6.p7
  91.6 0.0 copy-start.7
  91.6 0.0 collective-permute-done.5.p6
  91.6 0.0 copy-start.8
  91.6 0.0 collective-permute-done.4.p5
  91.6 0.0 copy-start.9
  91.6 0.6 copy-done.6
  92.3 0.1 copy-done.7
  92.4 0.1 copy-done.8
  92.5 0.1 copy-done.9
  92.5 20.0 %tail_part.1 = (bf16[2048,512]{1,0:T(8,128)(2,1)}, f32[1280,128]{1,0:T(8,128)}, f32[1280,128]{1,0:T(8,128)}) custom-call(s32[4]{0:T(128)} %pad_add_fusion.pos_ref, f32[2048,512]{1,0:T(8,128)} %get-tuple-element.13.agg_ref, bf16[2048,3072]{1,0:T(8,128)(2,1)} %get-tuple-element.14.rem_ref, f32[2048,512]{1,0:T(8,128)} %get-tuple-element.15.base_ref, ...), custom_call_target="tpu_custom_call" | custom-call | flops 10000000000 | bytes 30000000 | tf_op jit(solution)/shard_map/tail_part/pallas_call | solution.py:198
  112.5 0.4 collective-permute-start.7
  112.9 2.0 %collective-permute-done.7 = f32[1280,128]{1,0:T(8,128)S(1)} collective-permute-done((f32[1280,128]{1,0:T(8,128)}, f32[1280,128]{1,0:T(8,128)S(1)}, u32[]{:S(2)}, u32[]{:S(2)}) %collective-permute-start.7) | collective-permute-done | bytes 655392 | tf_op jit(solution)/shard_map/ppermute | solution.py:250
  114.9 1.2 add.78
  116.1 19.1 %all_to_all.28 = f32[16,80,128]{2,1,0:T(8,128)S(1)} all-to-all(f32[16,80,128]{2,1,0:T(8,128)S(1)} %bitcast.12), channel_id=1, replica_groups=mesh['y'=4,'core'=2,'z'=8,'x'=4] {'y','x'}, dimensions={0} | all-to-all | bytes 1310720 | tf_op jit(solution)/shard_map/all_to_all | solution.py:278
  135.3 15.2 %all_to_all.29 = f32[8,80,128]{2,1,0:T(8,128)S(1)} all-to-all(f32[8,80,128]{2,1,0:T(8,128)S(1)} %broadcast_in_dim.4), channel_id=1, replica_groups=mesh['y'=4,'core'=2,'z'=8,'x'=4] {'z'}, dimensions={0} | all-to-all | bytes 655360 | tf_op jit(solution)/shard_map/all_to_all | solution.py:278
  150.6 14.4 %all_to_all.30 = f32[16,80,128]{2,1,0:T(8,128)S(1)} all-to-all(f32[16,80,128]{2,1,0:T(8,128)S(1)} %broadcast_in_dim.5), channel_id=1, replica_groups=mesh['y'=4,'core'=2,'z'=8,'x'=4] {'y','x'}, dimensions={0} | all-to-all | bytes 1310720 | tf_op jit(solution)/shard_map/all_to_all | solution.py:278
  165.0 0.0 collective-permute-start.8
  165.0 2.1 %collective-permute-done.8.other_ref = f32[1280,128]{1,0:T(8,128)S(1)} collective-permute-done((f32[1280,128]{1,0:T(8,128)S(1)}, f32[1280,128]{1,0:T(8,128)S(1)}, u32[]{:S(2)}, u32[]{:S(2)}) %collective-permute-start.8) | collective-permute-done | bytes 655392 | tf_op jit(solution)/shard_map/ppermute | solution.py:250
  167.1 0.0 copy-done
  167.1 1.8 %unpack.1 = (f32[512,512]{1,0:T(8,128)}, f32[512,128]{1,0:T(8,128)}) custom-call(s32[4]{0:T(128)S(1)} %copy-done, f32[1280,128]{1,0:T(8,128)S(1)} %bitcast.11, f32[1280,128]{1,0:T(8,128)S(1)} %collective-permute-done.8.other_ref), custom_call_target="tpu_custom_call" | custom-call | tf_op jit(solution)/shard_map/unpack/pallas_call | solution.py:234
  (10 shorter events, 0.2 us)
Async XLA Ops:
  6.0 11.8 %copy-start.2 = (s32[2048,16]{0,1:T(8,128)S(1)}, s32[2048,16]{0,1:T(8,128)}, u32[]{:S(2)}) copy-start(s32[2048,16]{0,1:T(8,128)} %param.12) | copy-start | bytes 393220
  6.0 44.7 %all-to-all-start = ((bf16[32,40,512]{2,1,0:T(8,128)(2,1)}), bf16[32,40,512]{2,1,0:T(8,128)(2,1)S(1)}, u32[]{:S(2)}, u32[]{:S(2)}) async-start(bf16[32,40,512]{2,1,0:T(8,128)(2,1)} %pick_rows.1), calls=%async_computation | async-start | bytes 2621440 | tf_op jit(solution)/shard_map/all_to_all | solution.py:278
  50.7 32.0 %copy-start.1 = (bf16[32,40,512]{2,1,0:T(8,128)(2,1)}, bf16[32,40,512]{2,1,0:T(8,128)(2,1)S(1)}, u32[]{:S(2)}) copy-start(bf16[32,40,512]{2,1,0:T(8,128)(2,1)S(1)} %all-to-all-done) | copy-start | bytes 3932164
  50.7 32.6 %collective-permute-start.2 = (bf16[256,512]{1,0:T(8,128)(2,1)S(1)}, bf16[256,512]{1,0:T(8,128)(2,1)S(1)}, u32[]{:S(2)}, u32[]{:S(2)}) collective-permute-start(bf16[256,512]{1,0:T(8,128)(2,1)S(1)} %slice_bitcast_fusion), channel_id=1, source_target_pairs={{0,192},{64,0},{128,64},{192,128},{1,193},{65,1},{129,65},{193,129... | collective-permute-start | bytes 786440 | tf_op jit(solution)/shard_map/ppermute | solution.py:246
  53.8 30.0 %collective-permute-start.1 = (bf16[256,512]{1,0:T(8,128)(2,1)S(1)}, bf16[256,512]{1,0:T(8,128)(2,1)S(1)}, u32[]{:S(2)}, u32[]{:S(2)}) collective-permute-start(bf16[256,512]{1,0:T(8,128)(2,1)S(1)} %slice_bitcast_fusion), channel_id=1, source_target_pairs={{0,128},{64,192},{128,0},{192,64},{1,129},{65,193},{129,1},{193,65... | collective-permute-start | bytes 786440 | tf_op jit(solution)/shard_map/ppermute | solution.py:246
  54.4 29.5 %collective-permute-start = (bf16[256,512]{1,0:T(8,128)(2,1)S(1)}, bf16[256,512]{1,0:T(8,128)(2,1)S(1)}, u32[]{:S(2)}, u32[]{:S(2)}) collective-permute-start(bf16[256,512]{1,0:T(8,128)(2,1)S(1)} %slice_bitcast_fusion), channel_id=1, source_target_pairs={{0,64},{64,128},{128,192},{192,0},{1,65},{65,129},{129,193},{193,1... | collective-permute-start | bytes 786440 | tf_op jit(solution)/shard_map/ppermute | solution.py:246
  83.3 8.3 %collective-permute-start.3 = (bf16[256,512]{1,0:T(8,128)(2,1)S(1)}, bf16[256,512]{1,0:T(8,128)(2,1)S(1)}, u32[]{:S(2)}, u32[]{:S(2)}) collective-permute-start(bf16[256,512]{1,0:T(8,128)(2,1)S(1)} %slice_bitcast_fusion), channel_id=1, source_target_pairs={{0,32},{32,0},{1,33},{33,1},{2,34},{34,2},{3,35},{35,3},{4,36},{36... | collective-permute-start | bytes 786440 | tf_op jit(solution)/shard_map/ppermute | solution.py:250
  83.3 8.2 %copy-start.3 = (bf16[256,512]{1,0:T(8,128)(2,1)}, bf16[256,512]{1,0:T(8,128)(2,1)S(1)}, u32[]{:S(2)}) copy-start(bf16[256,512]{1,0:T(8,128)(2,1)S(1)} %collective-permute-done.2.p3) | copy-start | bytes 786436
  83.3 8.3 %collective-permute-start.6 = (bf16[256,512]{1,0:T(8,128)(2,1)S(1)}, bf16[256,512]{1,0:T(8,128)(2,1)S(1)}, u32[]{:S(2)}, u32[]{:S(2)}) collective-permute-start(bf16[256,512]{1,0:T(8,128)(2,1)S(1)} %collective-permute-done.2.p3), channel_id=1, source_target_pairs={{0,32},{32,0},{1,33},{33,1},{2,34},{34,2},{3,35},{35,3},{4,36},{36... | collective-permute-start | bytes 786440 | tf_op jit(solution)/shard_map/ppermute | solution.py:250
  83.8 7.7 %copy-start.4 = (bf16[256,512]{1,0:T(8,128)(2,1)}, bf16[256,512]{1,0:T(8,128)(2,1)S(1)}, u32[]{:S(2)}) copy-start(bf16[256,512]{1,0:T(8,128)(2,1)S(1)} %collective-permute-done.1.p2) | copy-start | bytes 786436
  83.8 7.8 %collective-permute-start.5 = (bf16[256,512]{1,0:T(8,128)(2,1)S(1)}, bf16[256,512]{1,0:T(8,128)(2,1)S(1)}, u32[]{:S(2)}, u32[]{:S(2)}) collective-permute-start(bf16[256,512]{1,0:T(8,128)(2,1)S(1)} %collective-permute-done.1.p2), channel_id=1, source_target_pairs={{0,32},{32,0},{1,33},{33,1},{2,34},{34,2},{3,35},{35,3},{4,36},{36... | collective-permute-start | bytes 786440 | tf_op jit(solution)/shard_map/ppermute | solution.py:250
  83.9 7.6 %copy-start.5 = (bf16[256,512]{1,0:T(8,128)(2,1)}, bf16[256,512]{1,0:T(8,128)(2,1)S(1)}, u32[]{:S(2)}) copy-start(bf16[256,512]{1,0:T(8,128)(2,1)S(1)} %collective-permute-done.p1) | copy-start | bytes 786436
  83.9 7.7 %collective-permute-start.4 = (bf16[256,512]{1,0:T(8,128)(2,1)S(1)}, bf16[256,512]{1,0:T(8,128)(2,1)S(1)}, u32[]{:S(2)}, u32[]{:S(2)}) collective-permute-start(bf16[256,512]{1,0:T(8,128)(2,1)S(1)} %collective-permute-done.p1), channel_id=1, source_target_pairs={{0,32},{32,0},{1,33},{33,1},{2,34},{34,2},{3,35},{35,3},{4,36},{36... | collective-permute-start | bytes 786440 | tf_op jit(solution)/shard_map/ppermute | solution.py:250
  91.6 0.7 copy-start.6
  91.6 0.8 copy-start.7
  91.6 0.9 copy-start.8
  91.6 0.9 copy-start.9
  112.5 2.4 %collective-permute-start.7 = (f32[1280,128]{1,0:T(8,128)}, f32[1280,128]{1,0:T(8,128)S(1)}, u32[]{:S(2)}, u32[]{:S(2)}) collective-permute-start(f32[1280,128]{1,0:T(8,128)} %get-tuple-element.20), channel_id=1, source_target_pairs={{0,32},{32,0},{1,33},{33,1},{2,34},{34,2},{3,35},{35,3},{4,36},{36... | collective-permute-start | bytes 1966088 | tf_op jit(solution)/shard_map/ppermute | solution.py:250
  135.2 31.9 %copy-start = (s32[4]{0:T(128)S(1)}, s32[4]{0:T(128)}, u32[]{:S(2)}) copy-start(s32[4]{0:T(128)} %pad_add_fusion.pos_ref) | copy-start | bytes 52
  165.0 2.1 %collective-permute-start.8 = (f32[1280,128]{1,0:T(8,128)S(1)}, f32[1280,128]{1,0:T(8,128)S(1)}, u32[]{:S(2)}, u32[]{:S(2)}) collective-permute-start(f32[1280,128]{1,0:T(8,128)S(1)} %bitcast.10), channel_id=1, source_target_pairs={{0,32},{32,0},{1,33},{33,1},{2,34},{34,2},{3,35},{35,3},{4,36},{36... | collective-permute-start | bytes 1966088 | tf_op jit(solution)/shard_map/ppermute | solution.py:250
where the time goes:
time: 171 us; the launch traced here: 169 us
  Pallas kernels  61.7 us (36%)
  blocking collectives  48.8 us (29%)
  waiting for transfers between devices  35 us (20%)
  starting transfers between devices  17.8 us (10%)
  local copies, waits for them, and re-layouts  2.42 us (1%)
  other arithmetic  2.4 us (1%)
    all_to_all x3, blocking collectives, a2a(): return lax.all_to_all(x, axes, split_axis=0, concat_axis=0, tiled=True)  48.8 us
    all_to_all x1, waiting for transfers between devices, a2a(): return lax.all_to_all(x, axes, split_axis=0, concat_axis=0, tiled=True)  30.9 us
    pallas_call x1, Pallas kernels, count_part(): pl.pallas_call(count_kernel, grid=(ROWS // TILE,), in_specs=[pl.BlockSpec...  27.3 us
    pallas_call x1, Pallas kernels, tail_part(): pl.pallas_call(functools.partial(tail_kernel, scale), grid=(ROWS // TILE,...  20 us
    all_to_all x1, starting transfers between devices, a2a(): return lax.all_to_all(x, axes, split_axis=0, concat_axis=0, tiled=True)  11.7 us
    pallas_call x1, Pallas kernels, dense_part(): pl.pallas_call(dense_kernel, grid=(ROWS // TILE,), in_specs=[tile(WIDTH),...  7.2 us
    pallas_call x1, Pallas kernels, pick_rows(): pl.pallas_call(pick_kernel, out_shape=jax.ShapeDtypeStruct((PEERS, SLOT,...  5.39 us
    ppermute x3, starting transfers between devices, shift(): return lax.ppermute(x, axis, [(i, (i + k) % n) for i in range(n)])  4.69 us
  transfers between devices with their start and end apart: 10, of which 3 were waited for; matrix products, arithmetic and copies ran while one was open for 2% of the time, Pallas kernels for 20%

commit v1 on v0

--- a/solution.py
+++ b/solution.py
@@ -25,14 +25,14 @@
 PEERS = 32
 CAP = 32
 HUBD = 8
-SLOT = CAP + HUBD
 LO = 256
 LOCAL_HI = ROWS // LO
 REM_HI = 12
 GROUP = 16
 TILE = 512
-VMEM = 60 << 20
-UNROLL = 2
+VMEM = 30 << 20
+UNROLL = 16
+FIRST = 1
 
 
 def onehot(cond):
@@ -47,35 +47,49 @@
     return pltpu.CompilerParams(vmem_limit_bytes=VMEM)
 
 
-def pick_kernel(rows_ref, hub_ref, x_ref, out_ref):
+def hub_kernel(hub_ref, x_ref, out_ref):
+    hub_t = hub_ref[...].T
+    lane = lax.broadcasted_iota(jnp.int32, (HUBD, ROWS), 1)
+    hubs = jnp.dot(onehot(hub_t[:, 0:1] == lane), x_ref[...], preferred_element_type=F32).astype(BF)
+    for s in range(PEERS):
+        out_ref[s] = hubs
+
+
+def halo_kernel(rows_ref, x_ref, out_ref):
     x = x_ref[...]
     rows_t = rows_ref[...].T
     lane = lax.broadcasted_iota(jnp.int32, (CAP, ROWS), 1)
     per = 8
-    hub_t = hub_ref[...].T
-    hub_lane = lax.broadcasted_iota(jnp.int32, (HUBD, ROWS), 1)
-    hubs = jnp.dot(onehot(hub_t[:, 0:1] == hub_lane), x, preferred_element_type=F32).astype(BF)
     for block in range(PEERS // per):
         picks = jnp.concatenate(
             [onehot(rows_t[:, s : s + 1] == lane) for s in range(block * per, (block + 1) * per)], axis=0
         )
         got = jnp.dot(picks, x, preferred_element_type=F32).astype(BF)
         for n in range(per):
-            out_ref[block * per + n, 0:CAP, :] = got[n * CAP : (n + 1) * CAP, :]
-            out_ref[block * per + n, CAP:SLOT, :] = hubs
-
-
-def pick_rows(feats, send_rows, hub_rows):
-    return pl.pallas_call(
-        pick_kernel,
-        out_shape=jax.ShapeDtypeStruct((PEERS, SLOT, WIDTH), BF),
+            out_ref[block * per + n] = got[n * CAP : (n + 1) * CAP, :]
+
+
+def hub_rows_of(feats, hub_rows):
+    return pl.pallas_call(
+        hub_kernel,
+        out_shape=pltpu.HBM((PEERS, HUBD, WIDTH), BF),
+        compiler_params=plain(),
+        name="hub_rows",
+    )(hub_rows, feats)
+
+
+def halo_rows_of(feats, send_rows):
+    return pl.pallas_call(
+        halo_kernel,
+        out_shape=pltpu.HBM((PEERS, CAP, WIDTH), BF),
         compiler_params=plain(),
         cost_estimate=pl.CostEstimate(flops=3_000_000_000, bytes_accessed=3_000_000, transcendentals=0),
-        name="pick_rows",
-    )(send_rows, hub_rows, feats)
-
-
-def count_kernel(idx_ref, xall_ref, agg_ref, rem_ref, loc_ref):
+        name="halo_rows",
+    )(send_rows, feats)
+
+
+def count_kernel(idx_ref, xall_ref, *refs):
+    agg_ref, rem_ref, loc_ref = refs[-3:]
     high = (LOCAL_HI + REM_HI) * GROUP
     left_row = lax.broadcasted_iota(jnp.int32, (high, LO), 0)
     low_row = lax.broadcasted_iota(jnp.int32, (LO, LO), 0)
@@ -83,8 +97,8 @@
 
     def build(g, carry):
         idx = idx_ref[pl.ds(g, 1), :]
-        where_hi = (idx // LO) * GROUP + node
-        where_lo = idx % LO
+        where_hi = (idx >> 8) * GROUP + node
+        where_lo = idx & (LO - 1)
         left = onehot(jnp.broadcast_to(where_hi, (high, LO)) == left_row)
         low = onehot(jnp.broadcast_to(where_lo, (LO, LO)) == low_row)
         counts = lax.dot_general(left, low, NT, preferred_element_type=F32).astype(BF)
@@ -100,19 +114,24 @@
     agg_ref[...] = jnp.dot(loc_ref[...], xall_ref[...], preferred_element_type=F32)
 
 
-def count_part(idx, feats):
+def count_part(idx, feats, at, steps, before):
     rem = REM_HI * LO
+    rows = lambda n: pl.BlockSpec((TILE, n), lambda i: (i + at, 0))
     return pl.pallas_call(
         count_kernel,
-        grid=(ROWS // TILE,),
-        in_specs=[pl.BlockSpec((TILE // GROUP, LO), lambda i: (i, 0)), whole((ROWS, WIDTH))],
-        out_specs=[tile(WIDTH), tile(rem)],
-        out_shape=[jax.ShapeDtypeStruct((ROWS, WIDTH), F32), jax.ShapeDtypeStruct((ROWS, rem), BF)],
+        grid=(steps,),
+        in_specs=[pl.BlockSpec((TILE // GROUP, LO), lambda i: (i + at, 0)), whole()]
+        + [pl.BlockSpec(memory_space=pl.ANY)] * len(before),
+        out_specs=[rows(WIDTH), rows(rem)],
+        out_shape=[pltpu.HBM((ROWS, WIDTH), F32), pltpu.HBM((ROWS, rem), BF)],
         scratch_shapes=[pltpu.VMEM((TILE, ROWS), BF)],
+        input_output_aliases={2: 0, 3: 1} if before else {},
         compiler_params=params(),
-        cost_estimate=pl.CostEstimate(flops=25_000_000_000, bytes_accessed=20_000_000, transcendentals=0),
+        cost_estimate=pl.CostEstimate(
+            flops=5_000_000_000 * steps, bytes_accessed=5_000_000 * steps, transcendentals=0
+        ),
         name="count_part",
-    )(idx, feats)
+    )(idx, feats, *before)
 
 
 def soft(logits):
@@ -129,8 +148,16 @@
     ps_ref[...] = soft(jnp.dot(hidden, ssecond_ref[...], preferred_element_type=F32))
 
 
-def whole(shape):
+def whole():
+    return pl.BlockSpec(memory_space=pltpu.VMEM)
+
+
+def once(shape):
     return pl.BlockSpec(shape, lambda i: (0,) * len(shape), pipeline_mode=pl.Buffered(1))
+
+
+def hbm(x):
+    return pltpu.with_memory_space_constraint(x, pltpu.HBM)
 
 
 def tile(n):
@@ -141,21 +168,17 @@
     return pl.pallas_call(
         dense_kernel,
         grid=(ROWS // TILE,),
-        in_specs=[tile(WIDTH), whole((WIDTH, WIDTH)), whole((WIDTH, WIDTH)), whole((WIDTH, 128))],
+        in_specs=[tile(WIDTH), whole(), whole(), whole()],
         out_specs=[tile(WIDTH), tile(WIDTH), tile(128)],
-        out_shape=[
-            jax.ShapeDtypeStruct((ROWS, WIDTH), F32),
-            jax.ShapeDtypeStruct((ROWS, WIDTH), BF),
-            jax.ShapeDtypeStruct((ROWS, 128), F32),
-        ],
+        out_shape=[pltpu.HBM((ROWS, WIDTH), F32), pltpu.HBM((ROWS, WIDTH), BF), pltpu.HBM((ROWS, 128), F32)],
         compiler_params=params(),
         cost_estimate=pl.CostEstimate(flops=3_000_000_000, bytes_accessed=10_000_000, transcendentals=0),
         name="dense_part",
-    )(feats, w_self, s_first, s_second)
+    )(hbm(feats), w_self, s_first, s_second)
 
 
 def tail_kernel(
-    scale, pos_ref, agg_ref, rem_ref, base_ref, sh_ref, ps_ref, x_ref, r_ref, p1, p2, p3, p4, p5, p6, p7,
+    scale, pos_ref, agg_ref, rem_ref, base_ref, sh_ref, ps_ref, x_ref, r_ref, p0, p1, p2, p3, p4, p5, p6, p7,
     wneigh_ref, whead_ref, ssecond_ref, hid_ref, keep_ref, send_ref, g_ref,
 ):
     step = pl.program_id(0)
@@ -164,9 +187,9 @@
     def _():
         g_ref[...] = jnp.zeros_like(g_ref)
 
-    first = PEERS * SLOT
+    first = PEERS * CAP
     acc = agg_ref[...] + jnp.dot(rem_ref[:, 0:first], r_ref[...], preferred_element_type=F32)
-    for n, part in enumerate((p1, p2, p3, p4, p5, p6, p7)):
+    for n, part in enumerate((p0, p1, p2, p3, p4, p5, p6, p7)):
         at = first + n * LO
         acc = acc + jnp.dot(rem_ref[:, at : at + LO], part[...], preferred_element_type=F32)
     agg = (acc / DEG).astype(BF)
@@ -200,13 +223,13 @@
         grid=(ROWS // TILE,),
         in_specs=[
             SMEM_SPEC, tile(WIDTH), tile(REM_HI * LO), tile(WIDTH), tile(WIDTH), tile(128), tile(WIDTH),
-            whole((PEERS * SLOT, WIDTH)),
+            once((PEERS * CAP, WIDTH)),
         ]
-        + [whole((LO, WIDTH))] * 7
-        + [whole((WIDTH, WIDTH)), whole((WIDTH, 128)), whole((WIDTH, 128))],
+        + [once((LO, WIDTH))] * 8
+        + [whole(), whole(), whole()],
         out_specs=[tile(WIDTH), fixed, fixed],
         out_shape=[
-            jax.ShapeDtypeStruct((ROWS, WIDTH), BF),
+            pltpu.HBM((ROWS, WIDTH), BF),
             jax.ShapeDtypeStruct((HALF, 128), F32),
             jax.ShapeDtypeStruct((HALF, 128), F32),
         ],
@@ -214,7 +237,7 @@
         compiler_params=params(),
         cost_estimate=pl.CostEstimate(flops=10_000_000_000, bytes_accessed=30_000_000, transcendentals=0),
         name="tail_part",
-    )(pos, agg, rem, base, sh, ps, feats, got, *parts, w_neigh, w_head, s_second)
+    )(pos, *map(hbm, (agg, rem, base, sh, ps, feats, got, *parts)), w_neigh, w_head, s_second)
 
 
 HALF = 5 * WIDTH // 2
@@ -261,16 +284,11 @@
 
 
 def remap(neighbours, y, c):
-    halo = neighbours - ROWS
-    halo_at = ROWS + (halo // CAP) * SLOT + halo % CAP
-    hub = halo - PEERS * CAP
-    inner = hub % LO
+    hub = neighbours - ROWS - PEERS * CAP
     block = hub // LO
     other = ((block % 2) ^ c) * NY + (y - block // 2) % NY
-    own_at = ROWS + (inner // HUBD) * SLOT + CAP + inner % HUBD
-    far_at = ROWS + PEERS * SLOT + (other - 1) * LO + inner
-    hub_at = jnp.where(other == 0, own_at, far_at)
-    out = jnp.where(halo < 0, neighbours, jnp.where(hub < 0, halo_at, hub_at))
+    far = ROWS + PEERS * CAP + other * LO + hub % LO
+    out = jnp.where(hub < 0, neighbours, far)
     return out.reshape(ROWS // GROUP, GROUP * DEG)
 
 
@@ -288,16 +306,17 @@
     pos = jnp.stack([y, c, lax.axis_index("z"), lax.axis_index("x")]).astype(jnp.int32)
     scale = 1.0 / float(ROWS * NY * NC * NZ * NX) ** 0.5
 
-    out = pick_rows(feats, send_rows[0], hub_rows)
+    own = a2a(hub_rows_of(feats, hub_rows), DOM).reshape(LO, WIDTH)
+    out = halo_rows_of(feats, send_rows[0])
     idx = remap(neighbours, y, c)
+    counts = count_part(idx, feats, 0, FIRST, [])
     got = a2a(out, DOM)
-    agg, rem = count_part(idx, feats)
-    own = got[:, CAP:SLOT, :].reshape(LO, WIDTH)
     ring = [own] + [shift(own, "y", NY, k) for k in range(1, NY)]
+    agg, rem = count_part(idx, feats, FIRST, ROWS // TILE - FIRST, counts)
+    cross = [swap(r) for r in ring]
     base, sh, ps = dense_part(feats, w_self, s_first, s_second)
-    cross = [swap(r) for r in ring]
     hidden, keep, send = tail_part(
-        scale, pos, agg, rem, base, sh, ps, feats, got.reshape(PEERS * SLOT, WIDTH), ring[1:] + cross,
+        scale, pos, agg, rem, base, sh, ps, feats, got.reshape(PEERS * CAP, WIDTH), ring + cross,
         w_neigh, w_head, s_second,
     )
     grad_first, grad_second = reduce_grads(pos, keep, send)

time: 171 us -> 143 us (0.84)
  waiting for transfers between devices: 35 us -> 9.77 us
  Pallas kernels: 61.7 us -> 49.2 us
  starting transfers between devices: 17.8 us -> 25 us
    all_to_all x1 -> x2, waiting for transfers between devices: 30.9 us -> 5.83 us  [a2a(): return lax.all_to_all(x, axes, split_axis=0, concat_axis=0, tiled=True)]
    pallas_call x2 -> x4, Pallas kernels: 32.7 us -> 21.2 us  [the longest x2 16.6 us: count_part(): pl.pallas_call(count_kernel, grid=(steps,), in_specs=[pl.BlockSpec((TILE...]
    all_to_all x1 -> x2, starting transfers between devices: 11.7 us -> 17.7 us  [a2a(): return lax.all_to_all(x, axes, split_axis=0, concat_axis=0, tiled=True)]
    unnamed x20 -> x26, local copies, waits for them, and re-layouts: 0.94 us -> 3.16 us
  transfers between devices with their start and end apart: 10 -> 11, of which waited for: 3 -> 3; matrix products, arithmetic and copies ran while one was open for 2% -> 1% of each run, Pallas kernels for 20% -> 19%
where the time goes in v1:
time: 143 us; the launch traced here: 140 us
  blocking collectives  50 us (35%)
  Pallas kernels  49.2 us (34%)
  starting transfers between devices  25 us (17%)
  waiting for transfers between devices  9.77 us (7%)
  local copies, waits for them, and re-layouts  4 us (3%)
  other arithmetic  1.43 us (1%)
    all_to_all x3, blocking collectives, a2a(): return lax.all_to_all(x, axes, split_axis=0, concat_axis=0, tiled=True)  50 us
    pallas_call x1, Pallas kernels, tail_part(): pl.pallas_call(functools.partial(tail_kernel, scale), grid=(ROWS // TILE,...  19.3 us
    all_to_all x2, starting transfers between devices, a2a(): return lax.all_to_all(x, axes, split_axis=0, concat_axis=0, tiled=True)  17.7 us
    pallas_call x2, Pallas kernels, count_part(): pl.pallas_call(count_kernel, grid=(steps,), in_specs=[pl.BlockSpec((TILE...  16.6 us
    pallas_call x1, Pallas kernels, dense_part(): pl.pallas_call(dense_kernel, grid=(ROWS // TILE,), in_specs=[tile(WIDTH),...  6.9 us
    all_to_all x2, waiting for transfers between devices, a2a(): return lax.all_to_all(x, axes, split_axis=0, concat_axis=0, tiled=True)  5.83 us
    ppermute x3, starting transfers between devices, shift(): return lax.ppermute(x, axis, [(i, (i + k) % n) for i in range(n)])  5.83 us
    ppermute x6, waiting for transfers between devices, swap(): return lax.ppermute(x, 'core', [(0, 1), (1, 0)])  3.93 us
  transfers between devices with their start and end apart: 11, of which 3 were waited for; matrix products, arithmetic and copies ran while one was open for 1% of the time, Pallas kernels for 19%

profile of v1, /device:TPU:2, one launch (start us, length us, event | category | flops | bytes accessed | tf_op | source)
XLA Modules:
  0.0 140.2 jit_solution(15613807242130805268)
XLA Ops:
  0.6 0.0 copy-start
  0.6 1.6 %copy-done = bf16[2048,512]{1,0:T(8,128)(2,1)S(1)} copy-done((bf16[2048,512]{1,0:T(8,128)(2,1)S(1)}, bf16[2048,512]{1,0:T(8,128)(2,1)}, u32[]{:S(2)}) %copy-start) | copy-done | bytes 2097176
  2.2 0.7 copy-done.2
  2.9 1.2 hub_rows.1
  4.1 11.7 %all-to-all-start.1 = ((bf16[32,8,512]{2,1,0:T(8,128)(2,1)}), bf16[32,8,512]{2,1,0:T(8,128)(2,1)}, u32[]{:S(2)}, u32[]{:S(2)}) async-start(bf16[32,8,512]{2,1,0:T(8,128)(2,1)} %hub_rows.1), calls=%async_computation.1 | async-start | bytes 524288 | tf_op jit(solution)/shard_map/all_to_all | solution.py:296
  15.8 1.2 fusion.6
  17.0 0.3 copy.16
  17.3 0.4 reshape.31.idx_ref
  17.8 0.0 copy-done.1
  17.8 0.0 copy-done.8
  17.8 3.4 %halo_rows.1 = bf16[32,32,512]{2,1,0:T(8,128)(2,1)} custom-call(s32[32,32]{1,0:T(8,128)S(1)} %bitcast.11, bf16[2048,512]{1,0:T(8,128)(2,1)S(1)} %copy-done.1), custom_call_target="tpu_custom_call" | custom-call | flops 3000000000 | bytes 3000000 | tf_op jit(solution)/shard_map/halo_rows/pallas_call | solution.py:82
  21.2 5.8 %all-to-all-done.1 = bf16[32,8,512]{2,1,0:T(8,128)(2,1)} async-done(((bf16[32,8,512]{2,1,0:T(8,128)(2,1)}), bf16[32,8,512]{2,1,0:T(8,128)(2,1)}, u32[]{:S(2)}, u32[]{:S(2)}) %all-to-all-start.1) | async-done | bytes 262176 | tf_op jit(solution)/shard_map/all_to_all | solution.py:296
  27.0 6.1 %all-to-all-start = ((bf16[32,32,512]{2,1,0:T(8,128)(2,1)}), bf16[32,32,512]{2,1,0:T(8,128)(2,1)}, u32[]{:S(2)}, u32[]{:S(2)}) async-start(bf16[32,32,512]{2,1,0:T(8,128)(2,1)} %halo_rows.1), calls=%async_computation | async-start | bytes 2097152 | tf_op jit(solution)/shard_map/all_to_all | solution.py:296
  33.1 5.1 %count_part.2 = (f32[2048,512]{1,0:T(8,128)}, bf16[2048,3072]{1,0:T(8,128)(2,1)}) custom-call(s32[128,256]{1,0:T(8,128)S(1)} %reshape.31.idx_ref, bf16[2048,512]{1,0:T(8,128)(2,1)S(1)} %copy-done.1), custom_call_target="tpu_custom_call" | custom-call | flops 5000000000 | bytes 5000000 | tf_op jit(solution)/shard_map/count_part/pallas_call | solution.py:120
  38.3 1.6 %collective-permute-start = (bf16[256,512]{1,0:T(8,128)(2,1)}, bf16[256,512]{1,0:T(8,128)(2,1)}, u32[]{:S(2)}, u32[]{:S(2)}) collective-permute-start(bf16[256,512]{1,0:T(8,128)(2,1)} %bitcast.6.p0), channel_id=1, source_target_pairs={{0,64},{64,128},{128,192},{192,0},{1,65},{65,129},{129,193},{193,1... | collective-permute-start | bytes 786440 | tf_op jit(solution)/shard_map/ppermute | solution.py:269
  39.8 2.9 %collective-permute-start.1 = (bf16[256,512]{1,0:T(8,128)(2,1)}, bf16[256,512]{1,0:T(8,128)(2,1)}, u32[]{:S(2)}, u32[]{:S(2)}) collective-permute-start(bf16[256,512]{1,0:T(8,128)(2,1)} %bitcast.6.p0), channel_id=1, source_target_pairs={{0,128},{64,192},{128,0},{192,64},{1,129},{65,193},{129,1},{193,65... | collective-permute-start | bytes 786440 | tf_op jit(solution)/shard_map/ppermute | solution.py:269
  42.7 1.3 collective-permute-start.2
  44.1 11.4 %count_part.3 = (f32[2048,512]{1,0:T(8,128)}, bf16[2048,3072]{1,0:T(8,128)(2,1)}) custom-call(s32[128,256]{1,0:T(8,128)S(1)} %reshape.31.idx_ref, bf16[2048,512]{1,0:T(8,128)(2,1)S(1)} %copy-done.1, f32[2048,512]{1,0:T(8,128)} %get-tuple-element.15.refs_0_, bf16[2048,3072]{1,0:T(8,128)(2,1)} %get-tuple-element.16.refs_1_), custom_call_target="tpu_custom_call", output_to_operand_aliasing={{0}: (2, {}), {1}: (3, {})} | custom-call | flops 15000000512 | bytes 15000000 | tf_op jit(solution)/shard_map/count_part/pallas_call | solution.py:120
  55.5 0.1 pad_add_fusion.pos_ref
  55.6 0.0 collective-permute-start.3
  55.7 0.0 collective-permute-done.p1
  55.7 0.5 collective-permute-start.4
  56.2 0.0 collective-permute-done.1.p2
  56.2 0.1 collective-permute-start.5
  56.3 0.0 collective-permute-done.2.p3
  56.3 0.4 collective-permute-start.6
  56.7 6.9 %dense_part.1 = (f32[2048,512]{1,0:T(8,128)}, bf16[2048,512]{1,0:T(8,128)(2,1)}, f32[2048,128]{1,0:T(8,128)}) custom-call(bf16[2048,512]{1,0:T(8,128)(2,1)} %x_ref.7, bf16[512,512]{1,0:T(8,128)(2,1)S(1)} %copy-done.3, bf16[512,512]{1,0:T(8,128)(2,1)S(1)} %copy-done.4, bf16[512,128]{1,0:T(8,128)(2,1)S(1)} %copy-done.6), custom_call_target="tpu_custom_call" | custom-call | flops 3000000000 | bytes 10000000 | tf_op jit(solution)/shard_map/dense_part/pallas_call | solution.py:168
  63.6 0.0 collective-permute-done.3.p4
  63.6 0.0 collective-permute-done.4.p5
  63.6 0.0 collective-permute-done.5.p6
  63.6 0.0 copy-start.11
  63.6 0.0 collective-permute-done.6.p7
  63.7 0.0 all-to-all-done
  63.7 0.6 copy-done.9
  64.3 0.1 copy-done.10
  64.4 0.1 copy-done.11
  64.5 0.1 copy-done.12
  64.6 0.0 copy-done.7
  64.6 19.3 %tail_part.1 = (bf16[2048,512]{1,0:T(8,128)(2,1)}, f32[1280,128]{1,0:T(8,128)S(1)}, f32[1280,128]{1,0:T(8,128)S(1)}) custom-call(s32[4]{0:T(128)S(1)} %pad_add_fusion.pos_ref, f32[2048,512]{1,0:T(8,128)} %get-tuple-element.17.agg_ref, bf16[2048,3072]{1,0:T(8,128)(2,1)} %get-tuple-element.18.rem_ref, f32[2048,512]{1,0:T(8,128)} %get-tuple-element.19.base_ref, ...), custom_call_target="tpu_custom_call" | custom-call | flops 10000000000 | bytes 30000000 | tf_op jit(solution)/shard_map/tail_part/pallas_call | solution.py:221
  83.8 0.4 collective-permute-start.7
  84.2 1.8 %collective-permute-done.7 = f32[1280,128]{1,0:T(8,128)S(1)} collective-permute-done((f32[1280,128]{1,0:T(8,128)S(1)}, f32[1280,128]{1,0:T(8,128)S(1)}, u32[]{:S(2)}, u32[]{:S(2)}) %collective-permute-start.7) | collective-permute-done | bytes 655392 | tf_op jit(solution)/shard_map/ppermute | solution.py:273
  86.0 0.1 add.42
  86.1 16.7 %all_to_all.33 = f32[16,80,128]{2,1,0:T(8,128)S(1)} all-to-all(f32[16,80,128]{2,1,0:T(8,128)S(1)} %bitcast.12), channel_id=1, replica_groups=mesh['y'=4,'core'=2,'z'=8,'x'=4] {'y','x'}, dimensions={0} | all-to-all | bytes 1310720 | tf_op jit(solution)/shard_map/all_to_all | solution.py:296
  102.9 19.2 %all_to_all.34 = f32[8,80,128]{2,1,0:T(8,128)S(1)} all-to-all(f32[8,80,128]{2,1,0:T(8,128)S(1)} %broadcast_in_dim.4), channel_id=1, replica_groups=mesh['y'=4,'core'=2,'z'=8,'x'=4] {'z'}, dimensions={0} | all-to-all | bytes 655360 | tf_op jit(solution)/shard_map/all_to_all | solution.py:296
  122.1 14.1 %all_to_all.35 = f32[16,80,128]{2,1,0:T(8,128)S(1)} all-to-all(f32[16,80,128]{2,1,0:T(8,128)S(1)} %broadcast_in_dim.5), channel_id=1, replica_groups=mesh['y'=4,'core'=2,'z'=8,'x'=4] {'y','x'}, dimensions={0} | all-to-all | bytes 1310720 | tf_op jit(solution)/shard_map/all_to_all | solution.py:296
  136.3 0.0 collective-permute-start.8
  136.3 2.1 %collective-permute-done.8.other_ref = f32[1280,128]{1,0:T(8,128)S(1)} collective-permute-done((f32[1280,128]{1,0:T(8,128)S(1)}, f32[1280,128]{1,0:T(8,128)S(1)}, u32[]{:S(2)}, u32[]{:S(2)}) %collective-permute-start.8) | collective-permute-done | bytes 655392 | tf_op jit(solution)/shard_map/ppermute | solution.py:273
  138.4 1.8 %unpack.1 = (f32[512,512]{1,0:T(8,128)}, f32[512,128]{1,0:T(8,128)}) custom-call(s32[4]{0:T(128)S(1)} %pad_add_fusion.pos_ref, f32[1280,128]{1,0:T(8,128)S(1)} %bitcast.10, f32[1280,128]{1,0:T(8,128)S(1)} %collective-permute-done.8.other_ref), custom_call_target="tpu_custom_call" | custom-call | tf_op jit(solution)/shard_map/unpack/pallas_call | solution.py:257
  (19 shorter events, 0.2 us)
Async XLA Ops:
  0.6 1.6 %copy-start = (bf16[2048,512]{1,0:T(8,128)(2,1)S(1)}, bf16[2048,512]{1,0:T(8,128)(2,1)}, u32[]{:S(2)}) copy-start(bf16[2048,512]{1,0:T(8,128)(2,1)} %x_ref.7) | copy-start | bytes 6291460
  2.2 0.7 copy-start.2
  2.9 14.9 %copy-start.1 = (bf16[2048,512]{1,0:T(8,128)(2,1)S(1)}, bf16[2048,512]{1,0:T(8,128)(2,1)}, u32[]{:S(2)}) copy-start(bf16[2048,512]{1,0:T(8,128)(2,1)} %x_ref.7) | copy-start | bytes 6291460
  2.9 14.9 %copy-start.8 = (s32[1,32,32]{2,1,0:T(8,128)S(1)}, s32[1,32,32]{2,1,0:T(8,128)}, u32[]{:S(2)}) copy-start(s32[1,32,32]{2,1,0:T(8,128)} %param.10) | copy-start | bytes 12292
  4.1 22.9 %all-to-all-start.1 = ((bf16[32,8,512]{2,1,0:T(8,128)(2,1)}), bf16[32,8,512]{2,1,0:T(8,128)(2,1)}, u32[]{:S(2)}, u32[]{:S(2)}) async-start(bf16[32,8,512]{2,1,0:T(8,128)(2,1)} %hub_rows.1), calls=%async_computation.1 | async-start | bytes 524288 | tf_op jit(solution)/shard_map/all_to_all | solution.py:296
  27.0 36.6 %all-to-all-start = ((bf16[32,32,512]{2,1,0:T(8,128)(2,1)}), bf16[32,32,512]{2,1,0:T(8,128)(2,1)}, u32[]{:S(2)}, u32[]{:S(2)}) async-start(bf16[32,32,512]{2,1,0:T(8,128)(2,1)} %halo_rows.1), calls=%async_computation | async-start | bytes 2097152 | tf_op jit(solution)/shard_map/all_to_all | solution.py:296
  38.3 17.4 %collective-permute-start = (bf16[256,512]{1,0:T(8,128)(2,1)}, bf16[256,512]{1,0:T(8,128)(2,1)}, u32[]{:S(2)}, u32[]{:S(2)}) collective-permute-start(bf16[256,512]{1,0:T(8,128)(2,1)} %bitcast.6.p0), channel_id=1, source_target_pairs={{0,64},{64,128},{128,192},{192,0},{1,65},{65,129},{129,193},{193,1... | collective-permute-start | bytes 786440 | tf_op jit(solution)/shard_map/ppermute | solution.py:269
  39.8 16.3 %collective-permute-start.1 = (bf16[256,512]{1,0:T(8,128)(2,1)}, bf16[256,512]{1,0:T(8,128)(2,1)}, u32[]{:S(2)}, u32[]{:S(2)}) collective-permute-start(bf16[256,512]{1,0:T(8,128)(2,1)} %bitcast.6.p0), channel_id=1, source_target_pairs={{0,128},{64,192},{128,0},{192,64},{1,129},{65,193},{129,1},{193,65... | collective-permute-start | bytes 786440 | tf_op jit(solution)/shard_map/ppermute | solution.py:269
  42.7 13.5 %collective-permute-start.2 = (bf16[256,512]{1,0:T(8,128)(2,1)}, bf16[256,512]{1,0:T(8,128)(2,1)}, u32[]{:S(2)}, u32[]{:S(2)}) collective-permute-start(bf16[256,512]{1,0:T(8,128)(2,1)} %bitcast.6.p0), channel_id=1, source_target_pairs={{0,192},{64,0},{128,64},{192,128},{1,193},{65,1},{129,65},{193,129... | collective-permute-start | bytes 786440 | tf_op jit(solution)/shard_map/ppermute | solution.py:269
  44.1 12.6 %copy-start.3 = (bf16[512,512]{1,0:T(8,128)(2,1)S(1)}, bf16[512,512]{1,0:T(8,128)(2,1)}, u32[]{:S(2)}) copy-start(bf16[512,512]{1,0:T(8,128)(2,1)} %wself_ref.1) | copy-start | bytes 1572868
  44.1 12.6 %copy-start.4 = (bf16[512,512]{1,0:T(8,128)(2,1)S(1)}, bf16[512,512]{1,0:T(8,128)(2,1)}, u32[]{:S(2)}) copy-start(bf16[512,512]{1,0:T(8,128)(2,1)} %sfirst_ref.1) | copy-start | bytes 1572868
  44.1 12.6 %copy-start.6 = (bf16[512,128]{1,0:T(8,128)(2,1)S(1)}, bf16[512,128]{1,0:T(8,128)(2,1)}, u32[]{:S(2)}) copy-start(bf16[512,128]{1,0:T(8,128)(2,1)} %ssecond_ref.3) | copy-start | bytes 393220
  55.6 9.0 %copy-start.5 = (bf16[512,512]{1,0:T(8,128)(2,1)S(1)}, bf16[512,512]{1,0:T(8,128)(2,1)}, u32[]{:S(2)}) copy-start(bf16[512,512]{1,0:T(8,128)(2,1)} %wneigh_ref.1) | copy-start | bytes 1572868
  55.6 9.0 %copy-start.7 = (bf16[512,128]{1,0:T(8,128)(2,1)S(1)}, bf16[512,128]{1,0:T(8,128)(2,1)}, u32[]{:S(2)}) copy-start(bf16[512,128]{1,0:T(8,128)(2,1)} %whead_ref.1) | copy-start | bytes 393220
  55.6 8.0 %collective-permute-start.3 = (bf16[256,512]{1,0:T(8,128)(2,1)}, bf16[256,512]{1,0:T(8,128)(2,1)S(1)}, u32[]{:S(2)}, u32[]{:S(2)}) collective-permute-start(bf16[256,512]{1,0:T(8,128)(2,1)} %bitcast.6.p0), channel_id=1, source_target_pairs={{0,32},{32,0},{1,33},{33,1},{2,34},{34,2},{3,35},{35,3},{4,36},{36... | collective-permute-start | bytes 786440 | tf_op jit(solution)/shard_map/ppermute | solution.py:273
  55.7 7.9 %collective-permute-start.4 = (bf16[256,512]{1,0:T(8,128)(2,1)}, bf16[256,512]{1,0:T(8,128)(2,1)S(1)}, u32[]{:S(2)}, u32[]{:S(2)}) collective-permute-start(bf16[256,512]{1,0:T(8,128)(2,1)} %collective-permute-done.p1), channel_id=1, source_target_pairs={{0,32},{32,0},{1,33},{33,1},{2,34},{34,2},{3,35},{35,3},{4,36},{36... | collective-permute-start | bytes 786440 | tf_op jit(solution)/shard_map/ppermute | solution.py:273
  56.2 7.4 %collective-permute-start.5 = (bf16[256,512]{1,0:T(8,128)(2,1)}, bf16[256,512]{1,0:T(8,128)(2,1)S(1)}, u32[]{:S(2)}, u32[]{:S(2)}) collective-permute-start(bf16[256,512]{1,0:T(8,128)(2,1)} %collective-permute-done.1.p2), channel_id=1, source_target_pairs={{0,32},{32,0},{1,33},{33,1},{2,34},{34,2},{3,35},{35,3},{4,36},{36... | collective-permute-start | bytes 786440 | tf_op jit(solution)/shard_map/ppermute | solution.py:273
  56.3 7.4 %collective-permute-start.6 = (bf16[256,512]{1,0:T(8,128)(2,1)}, bf16[256,512]{1,0:T(8,128)(2,1)S(1)}, u32[]{:S(2)}, u32[]{:S(2)}) collective-permute-start(bf16[256,512]{1,0:T(8,128)(2,1)} %collective-permute-done.2.p3), channel_id=1, source_target_pairs={{0,32},{32,0},{1,33},{33,1},{2,34},{34,2},{3,35},{35,3},{4,36},{36... | collective-permute-start | bytes 786440 | tf_op jit(solution)/shard_map/ppermute | solution.py:273
  63.6 0.7 copy-start.9
  63.6 0.8 copy-start.10
  63.6 0.9 copy-start.11
  63.6 0.9 copy-start.12
  83.8 2.2 %collective-permute-start.7 = (f32[1280,128]{1,0:T(8,128)S(1)}, f32[1280,128]{1,0:T(8,128)S(1)}, u32[]{:S(2)}, u32[]{:S(2)}) collective-permute-start(f32[1280,128]{1,0:T(8,128)S(1)} %get-tuple-element.24), channel_id=1, source_target_pairs={{0,32},{32,0},{1,33},{33,1},{2,34},{34,2},{3,35},{35,3},{4,36},{36... | collective-permute-start | bytes 1966088 | tf_op jit(solution)/shard_map/ppermute | solution.py:273
  136.3 2.1 %collective-permute-start.8 = (f32[1280,128]{1,0:T(8,128)S(1)}, f32[1280,128]{1,0:T(8,128)S(1)}, u32[]{:S(2)}, u32[]{:S(2)}) collective-permute-start(f32[1280,128]{1,0:T(8,128)S(1)} %bitcast.9), channel_id=1, source_target_pairs={{0,32},{32,0},{1,33},{33,1},{2,34},{34,2},{3,35},{35,3},{4,36},{36... | collective-permute-start | bytes 1966088 | tf_op jit(solution)/shard_map/ppermute | solution.py:273

commit v2 on v1

--- a/solution.py
+++ b/solution.py
@@ -10,10 +10,10 @@
 
 DEG = 16
 TEMPER = 2.0
-NY, NC, NZ, NX = 4, 2, 8, 4
-ALL = ("y", "core", "z", "x")
-DOM = ("z", "x")
-PLANE = ("y", "x")
+NY, NC, NZ, NP, NX = 4, 2, 4, 2, 4
+ALL = ("y", "core", "z", "pair", "x")
+DOM = ("z", "pair", "x")
+PLANE = ("y", "pair", "x")
 BF = jnp.bfloat16
 F32 = jnp.float32
 LAST = jnp.float32
@@ -28,6 +28,7 @@
 LO = 256
 LOCAL_HI = ROWS // LO
 REM_HI = 12
+FAR = 4
 GROUP = 16
 TILE = 512
 VMEM = 30 << 20
@@ -89,25 +90,36 @@
 
 
 def count_kernel(idx_ref, xall_ref, *refs):
-    agg_ref, rem_ref, loc_ref = refs[-3:]
+    agg_ref, rem_ref, ring_ref, loc_ref = refs[-4:]
     high = (LOCAL_HI + REM_HI) * GROUP
-    left_row = lax.broadcasted_iota(jnp.int32, (high, LO), 0)
-    low_row = lax.broadcasted_iota(jnp.int32, (LO, LO), 0)
+    row = lax.broadcasted_iota(jnp.int32, (LO, LO), 0).astype(F32).astype(BF)
+    over = high - LO
     node = lax.broadcasted_iota(jnp.int32, (1, LO), 1) // DEG
+    one = jnp.ones((LO, LO), BF)
+    zero = jnp.zeros((LO, LO), BF)
+
+    def spread(v, rows):
+        return jnp.broadcast_to(v.astype(F32).astype(BF), (rows, LO))
 
     def build(g, carry):
         idx = idx_ref[pl.ds(g, 1), :]
         where_hi = (idx >> 8) * GROUP + node
-        where_lo = idx & (LO - 1)
-        left = onehot(jnp.broadcast_to(where_hi, (high, LO)) == left_row)
-        low = onehot(jnp.broadcast_to(where_lo, (LO, LO)) == low_row)
+        left = jnp.concatenate(
+            [
+                jnp.where(spread(where_hi, LO) == row, one, zero),
+                jnp.where(spread(where_hi - LO, over) == row[0:over], one[0:over], zero[0:over]),
+            ],
+            axis=0,
+        )
+        low = jnp.where(spread(idx & (LO - 1), LO) == row, one, zero)
         counts = lax.dot_general(left, low, NT, preferred_element_type=F32).astype(BF)
         at = pl.ds(pl.multiple_of(g * GROUP, GROUP), GROUP)
         for h in range(LOCAL_HI):
             loc_ref[at, h * LO : (h + 1) * LO] = counts[h * GROUP : (h + 1) * GROUP, :]
         for h in range(REM_HI):
             r = (LOCAL_HI + h) * GROUP
-            rem_ref[at, h * LO : (h + 1) * LO] = counts[r : r + GROUP, :]
+            into, to = (ring_ref, h - FAR) if FAR <= h < 2 * FAR else (rem_ref, h % FAR + h // (2 * FAR) * FAR)
+            into[at, to * LO : (to + 1) * LO] = counts[r : r + GROUP, :]
         return carry
 
     lax.fori_loop(0, TILE // GROUP, build, 0, unroll=UNROLL)
@@ -115,17 +127,18 @@
 
 
 def count_part(idx, feats, at, steps, before):
-    rem = REM_HI * LO
     rows = lambda n: pl.BlockSpec((TILE, n), lambda i: (i + at, 0))
     return pl.pallas_call(
         count_kernel,
         grid=(steps,),
         in_specs=[pl.BlockSpec((TILE // GROUP, LO), lambda i: (i + at, 0)), whole()]
         + [pl.BlockSpec(memory_space=pl.ANY)] * len(before),
-        out_specs=[rows(WIDTH), rows(rem)],
-        out_shape=[pltpu.HBM((ROWS, WIDTH), F32), pltpu.HBM((ROWS, rem), BF)],
+        out_specs=[rows(WIDTH), rows(2 * FAR * LO), rows(FAR * LO)],
+        out_shape=[
+            pltpu.HBM((ROWS, WIDTH), F32), pltpu.HBM((ROWS, 2 * FAR * LO), BF), pltpu.HBM((ROWS, FAR * LO), BF),
+        ],
         scratch_shapes=[pltpu.VMEM((TILE, ROWS), BF)],
-        input_output_aliases={2: 0, 3: 1} if before else {},
+        input_output_aliases={2: 0, 3: 1, 4: 2} if before else {},
         compiler_params=params(),
         cost_estimate=pl.CostEstimate(
             flops=5_000_000_000 * steps, bytes_accessed=5_000_000 * steps, transcendentals=0
@@ -140,7 +153,13 @@
     return e / jnp.sum(e, axis=-1, keepdims=True)
 
 
-def dense_kernel(x_ref, wself_ref, sfirst_ref, ssecond_ref, base_ref, sh_ref, ps_ref):
+def dense_kernel(
+    agg_ref, ring_ref, x_ref, p0, p1, p2, p3, wself_ref, sfirst_ref, ssecond_ref, out_ref, base_ref, sh_ref, ps_ref
+):
+    acc = agg_ref[...]
+    for n, part in enumerate((p0, p1, p2, p3)):
+        acc = acc + jnp.dot(ring_ref[:, n * LO : (n + 1) * LO], part[...], preferred_element_type=F32)
+    out_ref[...] = acc
     x = x_ref[...]
     base_ref[...] = jnp.dot(x, wself_ref[...], preferred_element_type=F32)
     hidden = jnp.maximum(jnp.dot(x, sfirst_ref[...], preferred_element_type=F32), 0.0).astype(BF)
@@ -164,21 +183,26 @@
     return pl.BlockSpec((TILE, n), lambda i: (i, 0))
 
 
-def dense_part(feats, w_self, s_first, s_second):
+def dense_part(agg, ring, feats, parts, w_self, s_first, s_second):
     return pl.pallas_call(
         dense_kernel,
         grid=(ROWS // TILE,),
-        in_specs=[tile(WIDTH), whole(), whole(), whole()],
-        out_specs=[tile(WIDTH), tile(WIDTH), tile(128)],
-        out_shape=[pltpu.HBM((ROWS, WIDTH), F32), pltpu.HBM((ROWS, WIDTH), BF), pltpu.HBM((ROWS, 128), F32)],
+        in_specs=[tile(WIDTH), tile(FAR * LO), tile(WIDTH)]
+        + [once((LO, WIDTH))] * 4
+        + [whole(), whole(), whole()],
+        out_specs=[tile(WIDTH), tile(WIDTH), tile(WIDTH), tile(128)],
+        out_shape=[
+            pltpu.HBM((ROWS, WIDTH), F32), pltpu.HBM((ROWS, WIDTH), F32), pltpu.HBM((ROWS, WIDTH), BF),
+            pltpu.HBM((ROWS, 128), F32),
+        ],
         compiler_params=params(),
         cost_estimate=pl.CostEstimate(flops=3_000_000_000, bytes_accessed=10_000_000, transcendentals=0),
         name="dense_part",
-    )(hbm(feats), w_self, s_first, s_second)
+    )(*map(hbm, (agg, ring, feats, *parts)), w_self, s_first, s_second)
 
 
 def tail_kernel(
-    scale, pos_ref, agg_ref, rem_ref, base_ref, sh_ref, ps_ref, x_ref, r_ref, p0, p1, p2, p3, p4, p5, p6, p7,
+    scale, pos_ref, agg_ref, rem_ref, base_ref, sh_ref, ps_ref, x_ref, r_ref, p4, p5, p6, p7,
     wneigh_ref, whead_ref, ssecond_ref, hid_ref, keep_ref, send_ref, g_ref,
 ):
     step = pl.program_id(0)
@@ -189,7 +213,7 @@
 
     first = PEERS * CAP
     acc = agg_ref[...] + jnp.dot(rem_ref[:, 0:first], r_ref[...], preferred_element_type=F32)
-    for n, part in enumerate((p0, p1, p2, p3, p4, p5, p6, p7)):
+    for n, part in enumerate((p4, p5, p6, p7)):
         at = first + n * LO
         acc = acc + jnp.dot(rem_ref[:, at : at + LO], part[...], preferred_element_type=F32)
     agg = (acc / DEG).astype(BF)
@@ -222,10 +246,10 @@
         functools.partial(tail_kernel, scale),
         grid=(ROWS // TILE,),
         in_specs=[
-            SMEM_SPEC, tile(WIDTH), tile(REM_HI * LO), tile(WIDTH), tile(WIDTH), tile(128), tile(WIDTH),
+            SMEM_SPEC, tile(WIDTH), tile(2 * FAR * LO), tile(WIDTH), tile(WIDTH), tile(128), tile(WIDTH),
             once((PEERS * CAP, WIDTH)),
         ]
-        + [once((LO, WIDTH))] * 8
+        + [once((LO, WIDTH))] * 4
         + [whole(), whole(), whole()],
         out_specs=[tile(WIDTH), fixed, fixed],
         out_shape=[
@@ -275,7 +299,7 @@
 
 def reduce_grads(pos, keep, send):
     total = keep + swap(send)
-    plane = NY * NX
+    plane = NY * NP * NX
     piece = HALF // plane
     part = jnp.sum(a2a(total, PLANE).reshape(plane, piece, 128), axis=0)
     part = jnp.sum(a2a(copies(part, NZ), "z").reshape(NZ, piece, 128), axis=0)
@@ -303,8 +327,8 @@
 def body(feats, send_rows, hub_rows, neighbours, w_self, w_neigh, w_head, s_first, s_second):
     y = lax.axis_index("y")
     c = lax.axis_index("core")
-    pos = jnp.stack([y, c, lax.axis_index("z"), lax.axis_index("x")]).astype(jnp.int32)
-    scale = 1.0 / float(ROWS * NY * NC * NZ * NX) ** 0.5
+    pos = jnp.stack([y, c]).astype(jnp.int32)
+    scale = 1.0 / float(ROWS * NY * NC * NZ * NP * NX) ** 0.5
 
     own = a2a(hub_rows_of(feats, hub_rows), DOM).reshape(LO, WIDTH)
     out = halo_rows_of(feats, send_rows[0])
@@ -312,11 +336,11 @@
     counts = count_part(idx, feats, 0, FIRST, [])
     got = a2a(out, DOM)
     ring = [own] + [shift(own, "y", NY, k) for k in range(1, NY)]
-    agg, rem = count_part(idx, feats, FIRST, ROWS // TILE - FIRST, counts)
+    agg, rem, near = count_part(idx, feats, FIRST, ROWS // TILE - FIRST, counts)
     cross = [swap(r) for r in ring]
-    base, sh, ps = dense_part(feats, w_self, s_first, s_second)
+    agg, base, sh, ps = dense_part(agg, near, feats, ring, w_self, s_first, s_second)
     hidden, keep, send = tail_part(
-        scale, pos, agg, rem, base, sh, ps, feats, got.reshape(PEERS * CAP, WIDTH), ring + cross,
+        scale, pos, agg, rem, base, sh, ps, feats, got.reshape(PEERS * CAP, WIDTH), cross,
         w_neigh, w_head, s_second,
     )
     grad_first, grad_second = reduce_grads(pos, keep, send)
@@ -324,7 +348,7 @@
 
 
 def solution(mesh):
-    inner = Mesh(mesh.devices.reshape(NY, NC, NZ, NX), ALL)
+    inner = Mesh(mesh.devices.reshape(NY, NC, NZ, NP, NX), ALL)
     return jax.shard_map(
         body,
         mesh=inner,

time: 143 us -> 139 us (0.972)
  blocking collectives: 50 us -> 47.7 us
    pallas_call x1, Pallas kernels: 6.9 us -> 10.8 us  [dense_part(): pl.pallas_call(dense_kernel, grid=(ROWS // TILE,), in_specs=[tile(WIDTH),...]
    pallas_call x1, Pallas kernels: 19.3 us -> 16.2 us  [tail_part(): pl.pallas_call(functools.partial(tail_kernel, scale), grid=(ROWS // TILE,...]
    all_to_all x3, blocking collectives: 50 us -> 47.7 us  [a2a(): return lax.all_to_all(x, axes, split_axis=0, concat_axis=0, tiled=True)]
    pallas_call x2, Pallas kernels: 16.6 us -> 14.9 us  [count_part(): pl.pallas_call(count_kernel, grid=(steps,), in_specs=[pl.BlockSpec((TILE...]
    unnamed x26 -> x34, local copies, waits for them, and re-layouts: 3.16 us -> 3.83 us
  transfers between devices with their start and end apart: 11 -> 11, of which waited for: 3 -> 3; matrix products, arithmetic and copies ran while one was open for 1% -> 2% of each run, Pallas kernels for 19% -> 21%
where the time goes in v2:
time: 139 us; the launch traced here: 137 us
  Pallas kernels  48.3 us (35%)
  blocking collectives  47.7 us (34%)
  starting transfers between devices  24.5 us (18%)
  waiting for transfers between devices  9.67 us (7%)
  local copies, waits for them, and re-layouts  4.65 us (3%)
  other arithmetic  1.43 us (1%)
    all_to_all x3, blocking collectives, a2a(): return lax.all_to_all(x, axes, split_axis=0, concat_axis=0, tiled=True)  47.7 us
    all_to_all x2, starting transfers between devices, a2a(): return lax.all_to_all(x, axes, split_axis=0, concat_axis=0, tiled=True)  17.2 us
    pallas_call x1, Pallas kernels, tail_part(): pl.pallas_call(functools.partial(tail_kernel, scale), grid=(ROWS // TILE,...  16.2 us
    pallas_call x2, Pallas kernels, count_part(): pl.pallas_call(count_kernel, grid=(steps,), in_specs=[pl.BlockSpec((TILE...  14.9 us
    pallas_call x1, Pallas kernels, dense_part(): pl.pallas_call(dense_kernel, grid=(ROWS // TILE,), in_specs=[tile(WIDTH),...  10.8 us
    all_to_all x2, waiting for transfers between devices, a2a(): return lax.all_to_all(x, axes, split_axis=0, concat_axis=0, tiled=True)  5.83 us
    ppermute x3, starting transfers between devices, shift(): return lax.ppermute(x, axis, [(i, (i + k) % n) for i in range(n)])  5.82 us
    unnamed x34, local copies, waits for them, and re-layouts  3.83 us
  transfers between devices with their start and end apart: 11, of which 3 were waited for; matrix products, arithmetic and copies ran while one was open for 2% of the time, Pallas kernels for 21%

profile of v2, /device:TPU:2, one launch (start us, length us, event | category | flops | bytes accessed | tf_op | source)
XLA Modules:
  0.0 137.0 jit_solution(4156779847814500292)
XLA Ops:
  0.6 0.0 copy-start
  0.6 1.6 %copy-done = bf16[2048,512]{1,0:T(8,128)(2,1)S(1)} copy-done((bf16[2048,512]{1,0:T(8,128)(2,1)S(1)}, bf16[2048,512]{1,0:T(8,128)(2,1)}, u32[]{:S(2)}) %copy-start) | copy-done | bytes 2097176
  2.2 0.7 copy-done.5
  2.9 1.2 hub_rows.1
  4.1 11.7 %all-to-all-start = ((bf16[32,8,512]{2,1,0:T(8,128)(2,1)}), bf16[32,8,512]{2,1,0:T(8,128)(2,1)}, u32[]{:S(2)}, u32[]{:S(2)}) async-start(bf16[32,8,512]{2,1,0:T(8,128)(2,1)} %hub_rows.1), calls=%async_computation | async-start | bytes 524288 | tf_op jit(solution)/shard_map/all_to_all | solution.py:320
  15.8 1.2 fusion.6
  17.0 0.3 copy.17
  17.3 0.4 reshape.31.idx_ref
  17.8 3.4 %halo_rows.1 = bf16[32,32,512]{2,1,0:T(8,128)(2,1)} custom-call(s32[32,32]{1,0:T(8,128)S(1)} %bitcast.9, bf16[2048,512]{1,0:T(8,128)(2,1)S(1)} %copy-done.1), custom_call_target="tpu_custom_call" | custom-call | flops 3000000000 | bytes 3000000 | tf_op jit(solution)/shard_map/halo_rows/pallas_call | solution.py:83
  21.2 5.8 %all-to-all-done = bf16[32,8,512]{2,1,0:T(8,128)(2,1)} async-done(((bf16[32,8,512]{2,1,0:T(8,128)(2,1)}), bf16[32,8,512]{2,1,0:T(8,128)(2,1)}, u32[]{:S(2)}, u32[]{:S(2)}) %all-to-all-start) | async-done | bytes 262176 | tf_op jit(solution)/shard_map/all_to_all | solution.py:320
  27.0 5.6 %all-to-all-start.1 = ((bf16[32,32,512]{2,1,0:T(8,128)(2,1)}), bf16[32,32,512]{2,1,0:T(8,128)(2,1)S(1)}, u32[]{:S(2)}, u32[]{:S(2)}) async-start(bf16[32,32,512]{2,1,0:T(8,128)(2,1)} %halo_rows.1), calls=%async_computation.1 | async-start | bytes 2097152 | tf_op jit(solution)/shard_map/all_to_all | solution.py:320
  32.6 4.7 %count_part.2 = (f32[2048,512]{1,0:T(8,128)}, bf16[2048,2048]{1,0:T(8,128)(2,1)}, bf16[2048,1024]{1,0:T(8,128)(2,1)}) custom-call(s32[128,256]{1,0:T(8,128)S(1)} %reshape.31.idx_ref, bf16[2048,512]{1,0:T(8,128)(2,1)S(1)} %copy-done.1), custom_call_target="tpu_custom_call" | custom-call | flops 5000000000 | bytes 5000000 | tf_op jit(solution)/shard_map/count_part/pallas_call | solution.py:131
  37.3 1.6 %collective-permute-start = (bf16[256,512]{1,0:T(8,128)(2,1)}, bf16[256,512]{1,0:T(8,128)(2,1)S(1)}, u32[]{:S(2)}, u32[]{:S(2)}) collective-permute-start(bf16[256,512]{1,0:T(8,128)(2,1)} %bitcast.2.p0), channel_id=1, source_target_pairs={{0,64},{64,128},{128,192},{192,0},{1,65},{65,129},{129,193},{193,1... | collective-permute-start | bytes 786440 | tf_op jit(solution)/shard_map/ppermute | solution.py:293
  38.8 2.9 %collective-permute-start.1 = (bf16[256,512]{1,0:T(8,128)(2,1)}, bf16[256,512]{1,0:T(8,128)(2,1)S(1)}, u32[]{:S(2)}, u32[]{:S(2)}) collective-permute-start(bf16[256,512]{1,0:T(8,128)(2,1)} %bitcast.2.p0), channel_id=1, source_target_pairs={{0,128},{64,192},{128,0},{192,64},{1,129},{65,193},{129,1},{193,65... | collective-permute-start | bytes 786440 | tf_op jit(solution)/shard_map/ppermute | solution.py:293
  41.7 1.3 collective-permute-start.2
  43.1 10.3 %count_part.3 = (f32[2048,512]{1,0:T(8,128)}, bf16[2048,2048]{1,0:T(8,128)(2,1)}, bf16[2048,1024]{1,0:T(8,128)(2,1)}) custom-call(s32[128,256]{1,0:T(8,128)S(1)} %reshape.31.idx_ref, bf16[2048,512]{1,0:T(8,128)(2,1)S(1)} %copy-done.1, f32[2048,512]{1,0:T(8,128)} %get-tuple-element.18.refs_0_, ...), custom_call_target="tpu_custom_call", output_to_operand_aliasing={{0}: (2, {}), {1}: (3, {}), {2}: (4, {})} | custom-call | flops 15000000512 | bytes 15000000 | tf_op jit(solution)/shard_map/count_part/pallas_call | solution.py:131
  53.3 0.1 pad_add_fusion.pos_ref
  53.4 0.0 collective-permute-start.3
  53.5 0.0 collective-permute-done.p1
  53.5 0.0 copy-start.10
  53.5 0.5 collective-permute-start.4
  54.0 0.0 collective-permute-done.1.p2
  54.0 0.1 collective-permute-start.5
  54.1 0.0 collective-permute-done.2.p3
  54.1 0.4 collective-permute-start.6
  54.5 0.2 copy-done.11
  54.7 0.1 copy-done.12
  54.8 0.0 copy-start.7
  54.8 10.8 %dense_part.1 = (f32[2048,512]{1,0:T(8,128)}, f32[2048,512]{1,0:T(8,128)}, bf16[2048,512]{1,0:T(8,128)(2,1)}, f32[2048,128]{1,0:T(8,128)}) custom-call(f32[2048,512]{1,0:T(8,128)} %get-tuple-element.21.agg_ref, bf16[2048,1024]{1,0:T(8,128)(2,1)} %get-tuple-element.22.ring_ref, bf16[2048,512]{1,0:T(8,128)(2,1)} %x_ref.7, bf16[256,512]{1,0:T(8,128)(2,1)} %bitcast.2.p0, ...), custom_call_target="tpu_custom_call" | custom-call | flops 3000000000 | bytes 10000000 | tf_op jit(solution)/shard_map/dense_part/pallas_call | solution.py:187
  65.6 0.0 collective-permute-done.3.p4
  65.6 0.0 copy-start.13
  65.6 0.0 collective-permute-done.5.p6
  65.7 0.7 copy-done.14
  66.4 0.1 copy-done.15
  66.5 0.1 copy-done.16
  66.5 0.0 copy-done.13
  66.6 0.4 copy-done.9
  66.9 16.2 %tail_part.1 = (bf16[2048,512]{1,0:T(8,128)(2,1)}, f32[1280,128]{1,0:T(8,128)S(1)}, f32[1280,128]{1,0:T(8,128)S(1)}) custom-call(s32[2]{0:T(128)S(1)} %pad_add_fusion.pos_ref, f32[2048,512]{1,0:T(8,128)} %get-tuple-element.23.agg_ref, bf16[2048,2048]{1,0:T(8,128)(2,1)} %get-tuple-element.24.rem_ref, f32[2048,512]{1,0:T(8,128)} %get-tuple-element.25.base_ref, ...), custom_call_target="tpu_custom_call" | custom-call | flops 10000000000 | bytes 30000000 | tf_op jit(solution)/shard_map/tail_part/pallas_call | solution.py:245
  83.1 0.4 collective-permute-start.7
  83.5 1.7 %collective-permute-done.7 = f32[1280,128]{1,0:T(8,128)S(1)} collective-permute-done((f32[1280,128]{1,0:T(8,128)S(1)}, f32[1280,128]{1,0:T(8,128)S(1)}, u32[]{:S(2)}, u32[]{:S(2)}) %collective-permute-start.7) | collective-permute-done | bytes 655392 | tf_op jit(solution)/shard_map/ppermute | solution.py:297
  85.2 0.1 add.42
  85.3 18.5 %all_to_all.33 = f32[32,40,128]{2,1,0:T(8,128)S(1)} all-to-all(f32[32,40,128]{2,1,0:T(8,128)S(1)} %bitcast.10), channel_id=1, replica_groups=mesh['y'=4,'core'=2,'z'=4,'pair'=2,'x'=4] {'y','pair','x'}, dimensions={0} | all-to-all | bytes 1310720 | tf_op jit(solution)/shard_map/all_to_all | solution.py:320
  103.8 0.1 reduce_sum.18
  103.9 13.9 %all_to_all.34 = f32[4,40,128]{2,1,0:T(8,128)S(1)} all-to-all(f32[4,40,128]{2,1,0:T(8,128)S(1)} %broadcast_in_dim.4), channel_id=1, replica_groups=mesh['y'=4,'core'=2,'z'=4,'pair'=2,'x'=4] {'z'}, dimensions={0} | all-to-all | bytes 163840 | tf_op jit(solution)/shard_map/all_to_all | solution.py:320
  117.8 15.3 %all_to_all.35 = f32[32,40,128]{2,1,0:T(8,128)S(1)} all-to-all(f32[32,40,128]{2,1,0:T(8,128)S(1)} %broadcast_in_dim.5), channel_id=1, replica_groups=mesh['y'=4,'core'=2,'z'=4,'pair'=2,'x'=4] {'y','pair','x'}, dimensions={0} | all-to-all | bytes 1310720 | tf_op jit(solution)/shard_map/all_to_all | solution.py:320
  133.1 0.0 collective-permute-start.8
  133.1 2.1 %collective-permute-done.8.other_ref = f32[1280,128]{1,0:T(8,128)S(1)} collective-permute-done((f32[1280,128]{1,0:T(8,128)S(1)}, f32[1280,128]{1,0:T(8,128)S(1)}, u32[]{:S(2)}, u32[]{:S(2)}) %collective-permute-start.8) | collective-permute-done | bytes 655392 | tf_op jit(solution)/shard_map/ppermute | solution.py:297
  135.2 1.8 %unpack.1 = (f32[512,512]{1,0:T(8,128)}, f32[512,128]{1,0:T(8,128)}) custom-call(s32[2]{0:T(128)S(1)} %pad_add_fusion.pos_ref, f32[1280,128]{1,0:T(8,128)S(1)} %bitcast.8, f32[1280,128]{1,0:T(8,128)S(1)} %collective-permute-done.8.other_ref), custom_call_target="tpu_custom_call" | custom-call | tf_op jit(solution)/shard_map/unpack/pallas_call | solution.py:281
  (27 shorter events, 0.1 us)
Async XLA Ops:
  0.6 1.6 %copy-start = (bf16[2048,512]{1,0:T(8,128)(2,1)S(1)}, bf16[2048,512]{1,0:T(8,128)(2,1)}, u32[]{:S(2)}) copy-start(bf16[2048,512]{1,0:T(8,128)(2,1)} %x_ref.7) | copy-start | bytes 6291460
  2.2 0.7 copy-start.5
  2.9 14.9 %copy-start.1 = (bf16[2048,512]{1,0:T(8,128)(2,1)S(1)}, bf16[2048,512]{1,0:T(8,128)(2,1)}, u32[]{:S(2)}) copy-start(bf16[2048,512]{1,0:T(8,128)(2,1)} %x_ref.7) | copy-start | bytes 6291460
  2.9 14.9 %copy-start.8 = (s32[1,32,32]{2,1,0:T(8,128)S(1)}, s32[1,32,32]{2,1,0:T(8,128)}, u32[]{:S(2)}) copy-start(s32[1,32,32]{2,1,0:T(8,128)} %param.10) | copy-start | bytes 12292
  4.1 22.9 %all-to-all-start = ((bf16[32,8,512]{2,1,0:T(8,128)(2,1)}), bf16[32,8,512]{2,1,0:T(8,128)(2,1)}, u32[]{:S(2)}, u32[]{:S(2)}) async-start(bf16[32,8,512]{2,1,0:T(8,128)(2,1)} %hub_rows.1), calls=%async_computation | async-start | bytes 524288 | tf_op jit(solution)/shard_map/all_to_all | solution.py:320
  27.0 38.6 %all-to-all-start.1 = ((bf16[32,32,512]{2,1,0:T(8,128)(2,1)}), bf16[32,32,512]{2,1,0:T(8,128)(2,1)S(1)}, u32[]{:S(2)}, u32[]{:S(2)}) async-start(bf16[32,32,512]{2,1,0:T(8,128)(2,1)} %halo_rows.1), calls=%async_computation.1 | async-start | bytes 2097152 | tf_op jit(solution)/shard_map/all_to_all | solution.py:320
  37.3 16.2 %collective-permute-start = (bf16[256,512]{1,0:T(8,128)(2,1)}, bf16[256,512]{1,0:T(8,128)(2,1)S(1)}, u32[]{:S(2)}, u32[]{:S(2)}) collective-permute-start(bf16[256,512]{1,0:T(8,128)(2,1)} %bitcast.2.p0), channel_id=1, source_target_pairs={{0,64},{64,128},{128,192},{192,0},{1,65},{65,129},{129,193},{193,1... | collective-permute-start | bytes 786440 | tf_op jit(solution)/shard_map/ppermute | solution.py:293
  38.8 15.1 %collective-permute-start.1 = (bf16[256,512]{1,0:T(8,128)(2,1)}, bf16[256,512]{1,0:T(8,128)(2,1)S(1)}, u32[]{:S(2)}, u32[]{:S(2)}) collective-permute-start(bf16[256,512]{1,0:T(8,128)(2,1)} %bitcast.2.p0), channel_id=1, source_target_pairs={{0,128},{64,192},{128,0},{192,64},{1,129},{65,193},{129,1},{193,65... | collective-permute-start | bytes 786440 | tf_op jit(solution)/shard_map/ppermute | solution.py:293
  41.7 12.4 %collective-permute-start.2 = (bf16[256,512]{1,0:T(8,128)(2,1)}, bf16[256,512]{1,0:T(8,128)(2,1)S(1)}, u32[]{:S(2)}, u32[]{:S(2)}) collective-permute-start(bf16[256,512]{1,0:T(8,128)(2,1)} %bitcast.2.p0), channel_id=1, source_target_pairs={{0,192},{64,0},{128,64},{192,128},{1,193},{65,1},{129,65},{193,129... | collective-permute-start | bytes 786440 | tf_op jit(solution)/shard_map/ppermute | solution.py:293
  43.1 11.7 %copy-start.2 = (bf16[512,512]{1,0:T(8,128)(2,1)S(1)}, bf16[512,512]{1,0:T(8,128)(2,1)}, u32[]{:S(2)}) copy-start(bf16[512,512]{1,0:T(8,128)(2,1)} %wself_ref.1) | copy-start | bytes 1572868
  43.1 11.7 %copy-start.3 = (bf16[512,512]{1,0:T(8,128)(2,1)S(1)}, bf16[512,512]{1,0:T(8,128)(2,1)}, u32[]{:S(2)}) copy-start(bf16[512,512]{1,0:T(8,128)(2,1)} %sfirst_ref.1) | copy-start | bytes 1572868
  43.1 11.7 %copy-start.4 = (bf16[512,128]{1,0:T(8,128)(2,1)S(1)}, bf16[512,128]{1,0:T(8,128)(2,1)}, u32[]{:S(2)}) copy-start(bf16[512,128]{1,0:T(8,128)(2,1)} %ssecond_ref.3) | copy-start | bytes 393220
  53.4 12.2 %collective-permute-start.3 = (bf16[256,512]{1,0:T(8,128)(2,1)}, bf16[256,512]{1,0:T(8,128)(2,1)S(1)}, u32[]{:S(2)}, u32[]{:S(2)}) collective-permute-start(bf16[256,512]{1,0:T(8,128)(2,1)} %bitcast.2.p0), channel_id=1, source_target_pairs={{0,32},{32,0},{1,33},{33,1},{2,34},{34,2},{3,35},{35,3},{4,36},{36... | collective-permute-start | bytes 786440 | tf_op jit(solution)/shard_map/ppermute | solution.py:297
  53.5 1.0 copy-start.10
  53.5 12.1 %collective-permute-start.4 = (bf16[256,512]{1,0:T(8,128)(2,1)S(1)}, bf16[256,512]{1,0:T(8,128)(2,1)S(1)}, u32[]{:S(2)}, u32[]{:S(2)}) collective-permute-start(bf16[256,512]{1,0:T(8,128)(2,1)S(1)} %collective-permute-done.p1), channel_id=1, source_target_pairs={{0,32},{32,0},{1,33},{33,1},{2,34},{34,2},{3,35},{35,3},{4,36},{36... | collective-permute-start | bytes 786440 | tf_op jit(solution)/shard_map/ppermute | solution.py:297
  54.0 0.7 copy-start.11
  54.0 11.7 %collective-permute-start.5 = (bf16[256,512]{1,0:T(8,128)(2,1)S(1)}, bf16[256,512]{1,0:T(8,128)(2,1)S(1)}, u32[]{:S(2)}, u32[]{:S(2)}) collective-permute-start(bf16[256,512]{1,0:T(8,128)(2,1)S(1)} %collective-permute-done.1.p2), channel_id=1, source_target_pairs={{0,32},{32,0},{1,33},{33,1},{2,34},{34,2},{3,35},{35,3},{4,36},{36... | collective-permute-start | bytes 786440 | tf_op jit(solution)/shard_map/ppermute | solution.py:297
  54.1 0.7 copy-start.12
  54.1 11.6 %collective-permute-start.6 = (bf16[256,512]{1,0:T(8,128)(2,1)S(1)}, bf16[256,512]{1,0:T(8,128)(2,1)S(1)}, u32[]{:S(2)}, u32[]{:S(2)}) collective-permute-start(bf16[256,512]{1,0:T(8,128)(2,1)S(1)} %collective-permute-done.2.p3), channel_id=1, source_target_pairs={{0,32},{32,0},{1,33},{33,1},{2,34},{34,2},{3,35},{35,3},{4,36},{36... | collective-permute-start | bytes 786440 | tf_op jit(solution)/shard_map/ppermute | solution.py:297
  54.8 12.1 %copy-start.6 = (bf16[512,512]{1,0:T(8,128)(2,1)S(1)}, bf16[512,512]{1,0:T(8,128)(2,1)}, u32[]{:S(2)}) copy-start(bf16[512,512]{1,0:T(8,128)(2,1)} %wneigh_ref.1) | copy-start | bytes 1572868
  54.8 12.1 %copy-start.7 = (bf16[512,128]{1,0:T(8,128)(2,1)S(1)}, bf16[512,128]{1,0:T(8,128)(2,1)}, u32[]{:S(2)}) copy-start(bf16[512,128]{1,0:T(8,128)(2,1)} %whead_ref.1) | copy-start | bytes 393220
  65.6 1.0 copy-start.13
  65.6 0.8 copy-start.14
  65.6 0.8 copy-start.15
  65.7 0.9 copy-start.16
  65.7 1.3 copy-start.9
  83.1 2.1 %collective-permute-start.7 = (f32[1280,128]{1,0:T(8,128)S(1)}, f32[1280,128]{1,0:T(8,128)S(1)}, u32[]{:S(2)}, u32[]{:S(2)}) collective-permute-start(f32[1280,128]{1,0:T(8,128)S(1)} %get-tuple-element.30), channel_id=1, source_target_pairs={{0,32},{32,0},{1,33},{33,1},{2,34},{34,2},{3,35},{35,3},{4,36},{36... | collective-permute-start | bytes 1966088 | tf_op jit(solution)/shard_map/ppermute | solution.py:297
  133.1 2.1 %collective-permute-start.8 = (f32[1280,128]{1,0:T(8,128)S(1)}, f32[1280,128]{1,0:T(8,128)S(1)}, u32[]{:S(2)}, u32[]{:S(2)}) collective-permute-start(f32[1280,128]{1,0:T(8,128)S(1)} %bitcast.7), channel_id=1, source_target_pairs={{0,32},{32,0},{1,33},{33,1},{2,34},{34,2},{3,35},{35,3},{4,36},{36... | collective-permute-start | bytes 1966088 | tf_op jit(solution)/shard_map/ppermute | solution.py:297

commit v3 on v2

--- a/solution.py
+++ b/solution.py
@@ -16,7 +16,7 @@
 PLANE = ("y", "pair", "x")
 BF = jnp.bfloat16
 F32 = jnp.float32
-LAST = jnp.float32
+LAST = jnp.bfloat16
 NT = (((1,), (1,)), ((), ()))
 TN = (((0,), (0,)), ((), ()))
 
@@ -188,7 +188,7 @@
         dense_kernel,
         grid=(ROWS // TILE,),
         in_specs=[tile(WIDTH), tile(FAR * LO), tile(WIDTH)]
-        + [once((LO, WIDTH))] * 4
+        + [once((LO, WIDTH))] + [whole()] * 3
         + [whole(), whole(), whole()],
         out_specs=[tile(WIDTH), tile(WIDTH), tile(WIDTH), tile(128)],
         out_shape=[
@@ -198,7 +198,7 @@
         compiler_params=params(),
         cost_estimate=pl.CostEstimate(flops=3_000_000_000, bytes_accessed=10_000_000, transcendentals=0),
         name="dense_part",
-    )(*map(hbm, (agg, ring, feats, *parts)), w_self, s_first, s_second)
+    )(*map(hbm, (agg, ring, feats, parts[0])), *parts[1:], w_self, s_first, s_second)
 
 
 def tail_kernel(
@@ -247,9 +247,9 @@
         grid=(ROWS // TILE,),
         in_specs=[
             SMEM_SPEC, tile(WIDTH), tile(2 * FAR * LO), tile(WIDTH), tile(WIDTH), tile(128), tile(WIDTH),
-            once((PEERS * CAP, WIDTH)),
+            whole(),
         ]
-        + [once((LO, WIDTH))] * 4
+        + [once((LO, WIDTH))] + [whole()] * 3
         + [whole(), whole(), whole()],
         out_specs=[tile(WIDTH), fixed, fixed],
         out_shape=[
@@ -261,7 +261,7 @@
         compiler_params=params(),
         cost_estimate=pl.CostEstimate(flops=10_000_000_000, bytes_accessed=30_000_000, transcendentals=0),
         name="tail_part",
-    )(pos, *map(hbm, (agg, rem, base, sh, ps, feats, got, *parts)), w_neigh, w_head, s_second)
+    )(pos, *map(hbm, (agg, rem, base, sh, ps, feats)), got, hbm(parts[0]), *parts[1:], w_neigh, w_head, s_second)
 
 
 HALF = 5 * WIDTH // 2

time: 139 us -> 135 us (0.971)
  blocking collectives: 47.7 us -> 45.7 us
    all_to_all x3, blocking collectives: 47.7 us -> 45.7 us  [a2a(): return lax.all_to_all(x, axes, split_axis=0, concat_axis=0, tiled=True)]
    unnamed x34 -> x20, local copies, waits for them, and re-layouts: 3.83 us -> 2.92 us
  transfers between devices with their start and end apart: 11 -> 11, of which waited for: 3 -> 3; matrix products, arithmetic and copies ran while one was open for 2% -> 2% of each run, Pallas kernels for 21% -> 22%
where the time goes in v3:
time: 135 us; the launch traced here: 133 us
  Pallas kernels  47.9 us (35%)
  blocking collectives  45.7 us (34%)
  starting transfers between devices  24.4 us (18%)
  waiting for transfers between devices  9.3 us (7%)
  local copies, waits for them, and re-layouts  3.75 us (3%)
  other arithmetic  1.43 us (1%)
    all_to_all x3, blocking collectives, a2a(): return lax.all_to_all(x, axes, split_axis=0, concat_axis=0, tiled=True)  45.7 us
    all_to_all x2, starting transfers between devices, a2a(): return lax.all_to_all(x, axes, split_axis=0, concat_axis=0, tiled=True)  17.2 us
    pallas_call x1, Pallas kernels, tail_part(): pl.pallas_call(functools.partial(tail_kernel, scale), grid=(ROWS // TILE,...  15.7 us
    pallas_call x2, Pallas kernels, count_part(): pl.pallas_call(count_kernel, grid=(steps,), in_specs=[pl.BlockSpec((TILE...  14.9 us
    pallas_call x1, Pallas kernels, dense_part(): pl.pallas_call(dense_kernel, grid=(ROWS // TILE,), in_specs=[tile(WIDTH),...  10.9 us
    all_to_all x2, waiting for transfers between devices, a2a(): return lax.all_to_all(x, axes, split_axis=0, concat_axis=0, tiled=True)  5.83 us
    ppermute x3, starting transfers between devices, shift(): return lax.ppermute(x, axis, [(i, (i + k) % n) for i in range(n)])  5.82 us
    ppermute x6, waiting for transfers between devices, swap(): return lax.ppermute(x, 'core', [(0, 1), (1, 0)])  3.46 us
  transfers between devices with their start and end apart: 11, of which 3 were waited for; matrix products, arithmetic and copies ran while one was open for 2% of the time, Pallas kernels for 22%

profile of v3, /device:TPU:2, one launch (start us, length us, event | category | flops | bytes accessed | tf_op | source)
XLA Modules:
  0.0 133.2 jit_solution(2961512493798760447)
XLA Ops:
  0.6 0.0 copy-start
  0.6 1.6 %copy-done = bf16[2048,512]{1,0:T(8,128)(2,1)S(1)} copy-done((bf16[2048,512]{1,0:T(8,128)(2,1)S(1)}, bf16[2048,512]{1,0:T(8,128)(2,1)}, u32[]{:S(2)}) %copy-start) | copy-done | bytes 2097176
  2.2 0.7 copy-done.5
  2.9 1.2 hub_rows.1
  4.1 11.7 %all-to-all-start = ((bf16[32,8,512]{2,1,0:T(8,128)(2,1)}), bf16[32,8,512]{2,1,0:T(8,128)(2,1)}, u32[]{:S(2)}, u32[]{:S(2)}) async-start(bf16[32,8,512]{2,1,0:T(8,128)(2,1)} %hub_rows.1), calls=%async_computation | async-start | bytes 524288 | tf_op jit(solution)/shard_map/all_to_all | solution.py:320
  15.8 1.2 fusion.6
  17.0 0.3 copy.17
  17.3 0.4 reshape.33.idx_ref
  17.8 0.0 copy-done.1
  17.8 0.0 copy-done.8
  17.8 3.4 %halo_rows.1 = bf16[32,32,512]{2,1,0:T(8,128)(2,1)} custom-call(s32[32,32]{1,0:T(8,128)S(1)} %bitcast.10, bf16[2048,512]{1,0:T(8,128)(2,1)S(1)} %copy-done.1), custom_call_target="tpu_custom_call" | custom-call | flops 3000000000 | bytes 3000000 | tf_op jit(solution)/shard_map/halo_rows/pallas_call | solution.py:83
  21.2 5.8 %all-to-all-done = bf16[32,8,512]{2,1,0:T(8,128)(2,1)} async-done(((bf16[32,8,512]{2,1,0:T(8,128)(2,1)}), bf16[32,8,512]{2,1,0:T(8,128)(2,1)}, u32[]{:S(2)}, u32[]{:S(2)}) %all-to-all-start) | async-done | bytes 262176 | tf_op jit(solution)/shard_map/all_to_all | solution.py:320
  27.0 5.6 %all-to-all-start.1 = ((bf16[32,32,512]{2,1,0:T(8,128)(2,1)}), bf16[32,32,512]{2,1,0:T(8,128)(2,1)S(1)}, u32[]{:S(2)}, u32[]{:S(2)}) async-start(bf16[32,32,512]{2,1,0:T(8,128)(2,1)} %halo_rows.1), calls=%async_computation.1 | async-start | bytes 2097152 | tf_op jit(solution)/shard_map/all_to_all | solution.py:320
  32.6 4.7 %count_part.2 = (f32[2048,512]{1,0:T(8,128)}, bf16[2048,2048]{1,0:T(8,128)(2,1)}, bf16[2048,1024]{1,0:T(8,128)(2,1)}) custom-call(s32[128,256]{1,0:T(8,128)S(1)} %reshape.33.idx_ref, bf16[2048,512]{1,0:T(8,128)(2,1)S(1)} %copy-done.1), custom_call_target="tpu_custom_call" | custom-call | flops 5000000000 | bytes 5000000 | tf_op jit(solution)/shard_map/count_part/pallas_call | solution.py:131
  37.3 1.6 %collective-permute-start = (bf16[256,512]{1,0:T(8,128)(2,1)}, bf16[256,512]{1,0:T(8,128)(2,1)S(1)}, u32[]{:S(2)}, u32[]{:S(2)}) collective-permute-start(bf16[256,512]{1,0:T(8,128)(2,1)} %bitcast.2.p0), channel_id=1, source_target_pairs={{0,64},{64,128},{128,192},{192,0},{1,65},{65,129},{129,193},{193,1... | collective-permute-start | bytes 786440 | tf_op jit(solution)/shard_map/ppermute | solution.py:293
  38.8 2.9 %collective-permute-start.1 = (bf16[256,512]{1,0:T(8,128)(2,1)}, bf16[256,512]{1,0:T(8,128)(2,1)S(1)}, u32[]{:S(2)}, u32[]{:S(2)}) collective-permute-start(bf16[256,512]{1,0:T(8,128)(2,1)} %bitcast.2.p0), channel_id=1, source_target_pairs={{0,128},{64,192},{128,0},{192,64},{1,129},{65,193},{129,1},{193,65... | collective-permute-start | bytes 786440 | tf_op jit(solution)/shard_map/ppermute | solution.py:293
  41.7 1.3 %collective-permute-start.2 = (bf16[256,512]{1,0:T(8,128)(2,1)}, bf16[256,512]{1,0:T(8,128)(2,1)S(1)}, u32[]{:S(2)}, u32[]{:S(2)}) collective-permute-start(bf16[256,512]{1,0:T(8,128)(2,1)} %bitcast.2.p0), channel_id=1, source_target_pairs={{0,192},{64,0},{128,64},{192,128},{1,193},{65,1},{129,65},{193,129... | collective-permute-start | bytes 786440 | tf_op jit(solution)/shard_map/ppermute | solution.py:293
  43.1 10.3 %count_part.3 = (f32[2048,512]{1,0:T(8,128)}, bf16[2048,2048]{1,0:T(8,128)(2,1)}, bf16[2048,1024]{1,0:T(8,128)(2,1)}) custom-call(s32[128,256]{1,0:T(8,128)S(1)} %reshape.33.idx_ref, bf16[2048,512]{1,0:T(8,128)(2,1)S(1)} %copy-done.1, f32[2048,512]{1,0:T(8,128)} %get-tuple-element.18.refs_0_, ...), custom_call_target="tpu_custom_call", output_to_operand_aliasing={{0}: (2, {}), {1}: (3, {}), {2}: (4, {})} | custom-call | flops 15000000512 | bytes 15000000 | tf_op jit(solution)/shard_map/count_part/pallas_call | solution.py:131
  53.4 0.1 pad_add_fusion.pos_ref
  53.4 0.0 collective-permute-start.3
  53.5 0.0 collective-permute-done.p1
  53.5 0.5 collective-permute-start.4
  54.0 0.0 collective-permute-done.1.p2
  54.0 0.1 collective-permute-start.5
  54.1 0.0 collective-permute-done.2.p3
  54.1 0.4 collective-permute-start.6
  54.5 0.0 copy-done.2
  54.5 0.0 copy-done.3
  54.5 0.0 copy-start.7
  54.5 10.9 %dense_part.1 = (f32[2048,512]{1,0:T(8,128)}, f32[2048,512]{1,0:T(8,128)}, bf16[2048,512]{1,0:T(8,128)(2,1)}, f32[2048,128]{1,0:T(8,128)}) custom-call(f32[2048,512]{1,0:T(8,128)} %get-tuple-element.21.agg_ref, bf16[2048,1024]{1,0:T(8,128)(2,1)} %get-tuple-element.22.ring_ref, bf16[2048,512]{1,0:T(8,128)(2,1)} %x_ref.7, bf16[256,512]{1,0:T(8,128)(2,1)} %bitcast.2.p0, ...), custom_call_target="tpu_custom_call" | custom-call | flops 3000000000 | bytes 10000000 | tf_op jit(solution)/shard_map/dense_part/pallas_call | solution.py:187
  65.4 0.0 collective-permute-done.3.p4
  65.4 0.0 copy-start.9
  65.4 0.0 collective-permute-done.4.p5
  65.4 0.0 collective-permute-done.5.p6
  65.4 0.0 collective-permute-done.6.p7
  65.4 0.0 all-to-all-done.1
  65.4 0.7 copy-done.9
  66.1 15.7 %tail_part.1 = (bf16[2048,512]{1,0:T(8,128)(2,1)}, f32[1280,128]{1,0:T(8,128)S(1)}, f32[1280,128]{1,0:T(8,128)S(1)}) custom-call(s32[2]{0:T(128)S(1)} %pad_add_fusion.pos_ref, f32[2048,512]{1,0:T(8,128)} %get-tuple-element.23.agg_ref, bf16[2048,2048]{1,0:T(8,128)(2,1)} %get-tuple-element.24.rem_ref, f32[2048,512]{1,0:T(8,128)} %get-tuple-element.25.base_ref, ...), custom_call_target="tpu_custom_call" | custom-call | flops 10000000000 | bytes 30000000 | tf_op jit(solution)/shard_map/tail_part/pallas_call | solution.py:245
  81.8 0.3 collective-permute-start.7
  82.0 1.8 %collective-permute-done.7 = f32[1280,128]{1,0:T(8,128)S(1)} collective-permute-done((f32[1280,128]{1,0:T(8,128)S(1)}, f32[1280,128]{1,0:T(8,128)S(1)}, u32[]{:S(2)}, u32[]{:S(2)}) %collective-permute-start.7) | collective-permute-done | bytes 655392 | tf_op jit(solution)/shard_map/ppermute | solution.py:297
  83.9 0.1 add.42
  83.9 18.4 %all_to_all.33 = f32[32,40,128]{2,1,0:T(8,128)S(1)} all-to-all(f32[32,40,128]{2,1,0:T(8,128)S(1)} %bitcast.11), channel_id=1, replica_groups=mesh['y'=4,'core'=2,'z'=4,'pair'=2,'x'=4] {'y','pair','x'}, dimensions={0} | all-to-all | bytes 1310720 | tf_op jit(solution)/shard_map/all_to_all | solution.py:320
  102.3 0.1 reduce_sum.18
  102.4 13.9 %all_to_all.34 = f32[4,40,128]{2,1,0:T(8,128)S(1)} all-to-all(f32[4,40,128]{2,1,0:T(8,128)S(1)} %broadcast_in_dim.4), channel_id=1, replica_groups=mesh['y'=4,'core'=2,'z'=4,'pair'=2,'x'=4] {'z'}, dimensions={0} | all-to-all | bytes 163840 | tf_op jit(solution)/shard_map/all_to_all | solution.py:320
  116.4 13.4 %all_to_all.35 = bf16[32,40,128]{2,1,0:T(8,128)(2,1)S(1)} all-to-all(bf16[32,40,128]{2,1,0:T(8,128)(2,1)S(1)} %broadcast_in_dim.5), channel_id=1, replica_groups=mesh['y'=4,'core'=2,'z'=4,'pair'=2,'x'=4] {'y','pair','x'}, dimensions={0} | all-to-all | bytes 655360 | tf_op jit(solution)/shard_map/all_to_all | solution.py:320
  129.8 0.0 collective-permute-start.8
  129.8 1.6 %collective-permute-done.8.other_ref = bf16[1280,128]{1,0:T(8,128)(2,1)S(1)} collective-permute-done((bf16[1280,128]{1,0:T(8,128)(2,1)S(1)}, bf16[1280,128]{1,0:T(8,128)(2,1)S(1)}, u32[]{:S(2)}, u32[]{:S(2)}) %collective-permute-start.8) | collective-permute-done | bytes 327712 | tf_op jit(solution)/shard_map/ppermute | solution.py:297
  131.4 1.8 %unpack.1 = (f32[512,512]{1,0:T(8,128)}, f32[512,128]{1,0:T(8,128)}) custom-call(s32[2]{0:T(128)S(1)} %pad_add_fusion.pos_ref, bf16[1280,128]{1,0:T(8,128)(2,1)S(1)} %bitcast.8, bf16[1280,128]{1,0:T(8,128)(2,1)S(1)} %collective-permute-done.8.other_ref), custom_call_target="tpu_custom_call" | custom-call | tf_op jit(solution)/shard_map/unpack/pallas_call | solution.py:281
  (13 shorter events, 0.1 us)
Async XLA Ops:
  0.6 1.6 %copy-start = (bf16[2048,512]{1,0:T(8,128)(2,1)S(1)}, bf16[2048,512]{1,0:T(8,128)(2,1)}, u32[]{:S(2)}) copy-start(bf16[2048,512]{1,0:T(8,128)(2,1)} %x_ref.7) | copy-start | bytes 6291460
  2.2 0.7 copy-start.5
  2.9 14.9 %copy-start.1 = (bf16[2048,512]{1,0:T(8,128)(2,1)S(1)}, bf16[2048,512]{1,0:T(8,128)(2,1)}, u32[]{:S(2)}) copy-start(bf16[2048,512]{1,0:T(8,128)(2,1)} %x_ref.7) | copy-start | bytes 6291460
  2.9 14.9 %copy-start.8 = (s32[1,32,32]{2,1,0:T(8,128)S(1)}, s32[1,32,32]{2,1,0:T(8,128)}, u32[]{:S(2)}) copy-start(s32[1,32,32]{2,1,0:T(8,128)} %param.10) | copy-start | bytes 12292
  4.1 22.9 %all-to-all-start = ((bf16[32,8,512]{2,1,0:T(8,128)(2,1)}), bf16[32,8,512]{2,1,0:T(8,128)(2,1)}, u32[]{:S(2)}, u32[]{:S(2)}) async-start(bf16[32,8,512]{2,1,0:T(8,128)(2,1)} %hub_rows.1), calls=%async_computation | async-start | bytes 524288 | tf_op jit(solution)/shard_map/all_to_all | solution.py:320
  27.0 38.4 %all-to-all-start.1 = ((bf16[32,32,512]{2,1,0:T(8,128)(2,1)}), bf16[32,32,512]{2,1,0:T(8,128)(2,1)S(1)}, u32[]{:S(2)}, u32[]{:S(2)}) async-start(bf16[32,32,512]{2,1,0:T(8,128)(2,1)} %halo_rows.1), calls=%async_computation.1 | async-start | bytes 2097152 | tf_op jit(solution)/shard_map/all_to_all | solution.py:320
  37.3 16.2 %collective-permute-start = (bf16[256,512]{1,0:T(8,128)(2,1)}, bf16[256,512]{1,0:T(8,128)(2,1)S(1)}, u32[]{:S(2)}, u32[]{:S(2)}) collective-permute-start(bf16[256,512]{1,0:T(8,128)(2,1)} %bitcast.2.p0), channel_id=1, source_target_pairs={{0,64},{64,128},{128,192},{192,0},{1,65},{65,129},{129,193},{193,1... | collective-permute-start | bytes 786440 | tf_op jit(solution)/shard_map/ppermute | solution.py:293
  38.8 15.1 %collective-permute-start.1 = (bf16[256,512]{1,0:T(8,128)(2,1)}, bf16[256,512]{1,0:T(8,128)(2,1)S(1)}, u32[]{:S(2)}, u32[]{:S(2)}) collective-permute-start(bf16[256,512]{1,0:T(8,128)(2,1)} %bitcast.2.p0), channel_id=1, source_target_pairs={{0,128},{64,192},{128,0},{192,64},{1,129},{65,193},{129,1},{193,65... | collective-permute-start | bytes 786440 | tf_op jit(solution)/shard_map/ppermute | solution.py:293
  41.7 12.4 %collective-permute-start.2 = (bf16[256,512]{1,0:T(8,128)(2,1)}, bf16[256,512]{1,0:T(8,128)(2,1)S(1)}, u32[]{:S(2)}, u32[]{:S(2)}) collective-permute-start(bf16[256,512]{1,0:T(8,128)(2,1)} %bitcast.2.p0), channel_id=1, source_target_pairs={{0,192},{64,0},{128,64},{192,128},{1,193},{65,1},{129,65},{193,129... | collective-permute-start | bytes 786440 | tf_op jit(solution)/shard_map/ppermute | solution.py:293
  43.1 11.4 %copy-start.2 = (bf16[512,512]{1,0:T(8,128)(2,1)S(1)}, bf16[512,512]{1,0:T(8,128)(2,1)}, u32[]{:S(2)}) copy-start(bf16[512,512]{1,0:T(8,128)(2,1)} %wself_ref.1) | copy-start | bytes 1572868
  43.1 11.4 %copy-start.3 = (bf16[512,512]{1,0:T(8,128)(2,1)S(1)}, bf16[512,512]{1,0:T(8,128)(2,1)}, u32[]{:S(2)}) copy-start(bf16[512,512]{1,0:T(8,128)(2,1)} %sfirst_ref.1) | copy-start | bytes 1572868
  43.1 11.4 %copy-start.4 = (bf16[512,128]{1,0:T(8,128)(2,1)S(1)}, bf16[512,128]{1,0:T(8,128)(2,1)}, u32[]{:S(2)}) copy-start(bf16[512,128]{1,0:T(8,128)(2,1)} %ssecond_ref.3) | copy-start | bytes 393220
  53.4 11.9 %collective-permute-start.3 = (bf16[256,512]{1,0:T(8,128)(2,1)}, bf16[256,512]{1,0:T(8,128)(2,1)S(1)}, u32[]{:S(2)}, u32[]{:S(2)}) collective-permute-start(bf16[256,512]{1,0:T(8,128)(2,1)} %bitcast.2.p0), channel_id=1, source_target_pairs={{0,32},{32,0},{1,33},{33,1},{2,34},{34,2},{3,35},{35,3},{4,36},{36... | collective-permute-start | bytes 786440 | tf_op jit(solution)/shard_map/ppermute | solution.py:297
  53.5 11.9 %collective-permute-start.4 = (bf16[256,512]{1,0:T(8,128)(2,1)S(1)}, bf16[256,512]{1,0:T(8,128)(2,1)S(1)}, u32[]{:S(2)}, u32[]{:S(2)}) collective-permute-start(bf16[256,512]{1,0:T(8,128)(2,1)S(1)} %collective-permute-done.p1), channel_id=1, source_target_pairs={{0,32},{32,0},{1,33},{33,1},{2,34},{34,2},{3,35},{35,3},{4,36},{36... | collective-permute-start | bytes 786440 | tf_op jit(solution)/shard_map/ppermute | solution.py:297
  54.0 11.4 %collective-permute-start.5 = (bf16[256,512]{1,0:T(8,128)(2,1)S(1)}, bf16[256,512]{1,0:T(8,128)(2,1)S(1)}, u32[]{:S(2)}, u32[]{:S(2)}) collective-permute-start(bf16[256,512]{1,0:T(8,128)(2,1)S(1)} %collective-permute-done.1.p2), channel_id=1, source_target_pairs={{0,32},{32,0},{1,33},{33,1},{2,34},{34,2},{3,35},{35,3},{4,36},{36... | collective-permute-start | bytes 786440 | tf_op jit(solution)/shard_map/ppermute | solution.py:297
  54.1 11.3 %collective-permute-start.6 = (bf16[256,512]{1,0:T(8,128)(2,1)S(1)}, bf16[256,512]{1,0:T(8,128)(2,1)S(1)}, u32[]{:S(2)}, u32[]{:S(2)}) collective-permute-start(bf16[256,512]{1,0:T(8,128)(2,1)S(1)} %collective-permute-done.2.p3), channel_id=1, source_target_pairs={{0,32},{32,0},{1,33},{33,1},{2,34},{34,2},{3,35},{35,3},{4,36},{36... | collective-permute-start | bytes 786440 | tf_op jit(solution)/shard_map/ppermute | solution.py:297
  54.5 11.6 %copy-start.6 = (bf16[512,512]{1,0:T(8,128)(2,1)S(1)}, bf16[512,512]{1,0:T(8,128)(2,1)}, u32[]{:S(2)}) copy-start(bf16[512,512]{1,0:T(8,128)(2,1)} %wneigh_ref.1) | copy-start | bytes 1572868
  54.5 11.6 %copy-start.7 = (bf16[512,128]{1,0:T(8,128)(2,1)S(1)}, bf16[512,128]{1,0:T(8,128)(2,1)}, u32[]{:S(2)}) copy-start(bf16[512,128]{1,0:T(8,128)(2,1)} %whead_ref.1) | copy-start | bytes 393220
  65.4 0.7 copy-start.9
  81.8 2.1 %collective-permute-start.7 = (f32[1280,128]{1,0:T(8,128)S(1)}, f32[1280,128]{1,0:T(8,128)S(1)}, u32[]{:S(2)}, u32[]{:S(2)}) collective-permute-start(f32[1280,128]{1,0:T(8,128)S(1)} %get-tuple-element.30), channel_id=1, source_target_pairs={{0,32},{32,0},{1,33},{33,1},{2,34},{34,2},{3,35},{35,3},{4,36},{36... | collective-permute-start | bytes 1966088 | tf_op jit(solution)/shard_map/ppermute | solution.py:297
  129.8 1.6 %collective-permute-start.8 = (bf16[1280,128]{1,0:T(8,128)(2,1)S(1)}, bf16[1280,128]{1,0:T(8,128)(2,1)S(1)}, u32[]{:S(2)}, u32[]{:S(2)}) collective-permute-start(bf16[1280,128]{1,0:T(8,128)(2,1)S(1)} %bitcast.7), channel_id=1, source_target_pairs={{0,32},{32,0},{1,33},{33,1},{2,34},{34,2},{3,35},{35,3},{4,36},{36... | collective-permute-start | bytes 983048 | tf_op jit(solution)/shard_map/ppermute | solution.py:297
